TPU v7x, 1024 devices: a whole 4x8x16 slice. The times are simulated.
1024 devices in a mesh: seq: 64 (over z, y_hi), fsdp: 8 (over x, core), canvas: 2 (over y_lo).
Axes of the slice: x: 4, y: 8 (y_hi: 4, y_lo: 2; y = y_hi * 2 + y_lo), z: 16, core: 2. Of those that a mesh axis runs over, the one named last changes fastest.
Arguments:
- patch_tokens: bfloat16 [8, 16384, 1024], P('fsdp', 'seq'), may hold values from -6 to 6
- keep_mask: int32 [8, 16384], P('fsdp', 'seq'), may hold values from 0 to 1, as said below
- slot_index: int32 [8, 16384], P('fsdp', 'seq'), may hold values from 0 to 8191, as said below
- tile_map: int32 [8, 1024], P('fsdp', 'seq'), may hold values from 0 to 1023, each once within a row
- qkv_proj: bfloat16 [1024, 2, 3, 512], P(None, 'canvas'), may hold values from -1 to 1
- out_proj: bfloat16 [1024, 1024], replicated, may hold values from -0.1875 to 0.1875
- up_proj: bfloat16 [1024, 4096], P('fsdp', 'canvas'), may hold values from -0.1875 to 0.1875
- down_proj: bfloat16 [1024, 4096], P('fsdp', 'canvas'), may hold values from -0.09375 to 0.09375
Outputs:
- encoded: bfloat16 [8, 8192, 1024], P('fsdp', ('seq', 'canvas'))
Inputs may be any that keep to these rules, and one draw needn't show every extreme that they name: Exactly 8192 tokens of each scene have keep_mask 1. Over the kept tokens of a scene, slot_index takes every value below 8192 once. The kept tokens of one index of seq whose slots fall in one block of 128 slots fill one whole aligned run of 4 slots; each block is filled by runs from 32 indices of seq. `tile_map`: each canvas tile of a scene appears once.
All inputs are finite; a program needn't handle non-finite values.
Results may differ from a plain program's by a relative error of at most 0.0085.
Values may be sent and summed in bfloat16 or wider, within the bound.
A program may use at most 64 MiB of HBM per device.

v0:
```python
import jax
import jax.numpy as jnp
from jax import lax
from jax.sharding import PartitionSpec as P

D = 1024
HEAD_DIM = 64
TILE_SIDE = 4
TILES_W = 32


EPS = 1e-06


def passed_along(value, axis, steps):
    count = lax.axis_size(axis)
    pairs = [(source, (source + steps) % count) for source in range(count)]
    return lax.ppermute(value, axis, pairs)


def layer_norm(values):
    centered = values - jnp.mean(values, axis=-1, keepdims=True)
    spread = jnp.mean(centered * centered, axis=-1, keepdims=True)
    return centered * lax.rsqrt(spread + EPS)


def position_table(tile_ids):
    tile_count = tile_ids.shape[0]
    tile_size = TILE_SIDE * TILE_SIDE
    tile_cell = jnp.repeat(tile_ids, tile_size)
    within = jnp.arange(tile_count * tile_size, dtype=jnp.int32) % tile_size
    row_at = tile_cell // TILES_W * TILE_SIDE + within // TILE_SIDE
    col_at = tile_cell % TILES_W * TILE_SIDE + within % TILE_SIDE
    quarter = D // 4
    frequency = 10000.0 ** (-jnp.arange(quarter, dtype=jnp.float32) / quarter)
    row_angle = row_at.astype(jnp.float32)[:, None] * frequency[None, :]
    col_angle = col_at.astype(jnp.float32)[:, None] * frequency[None, :]
    return jnp.concatenate(
        [jnp.sin(row_angle), jnp.cos(row_angle), jnp.sin(col_angle), jnp.cos(col_angle)], axis=1
    )


def attend_block(queries, pairs_here, pairs_prev, group_w):
    heads_here = group_w // HEAD_DIM
    row_count = queries.shape[0]
    pairs_all = jnp.concatenate([pairs_here, pairs_prev], axis=0)
    keys_all = pairs_all[:, :group_w].reshape(2 * row_count, heads_here, HEAD_DIM)
    values_all = pairs_all[:, group_w:].reshape(2 * row_count, heads_here, HEAD_DIM)
    query_heads = queries.reshape(row_count, heads_here, HEAD_DIM)
    scores = jnp.einsum(
        "qhe,khe->hqk", query_heads, keys_all, preferred_element_type=jnp.float32
    ) * HEAD_DIM ** (-0.5)
    row_peak = jnp.max(scores, axis=-1, keepdims=True)
    expo_terms = jnp.exp(scores - row_peak)
    row_total = jnp.sum(expo_terms, axis=-1)
    probs = expo_terms.astype(jnp.bfloat16)
    summed = jnp.einsum("hqk,khe->qhe", probs, values_all, preferred_element_type=jnp.float32)
    attended = summed / jnp.transpose(row_total)[:, :, None]
    return attended.astype(jnp.bfloat16).reshape(row_count, group_w)


def shards(patch_tokens, keep_mask, slot_index, tile_map, qkv_proj, out_proj, up_proj, down_proj):
    seq_count = lax.axis_size("seq")
    pair_here = lax.axis_index("canvas")
    tok_dev = patch_tokens.shape[1]
    vis_dev = tok_dev // 2
    run_length = 2 * vis_dev // seq_count
    embedded = (patch_tokens[0].astype(jnp.float32) + position_table(tile_map[0])).astype(
        jnp.bfloat16
    )
    kept_here = keep_mask[0] == 1
    slot_here = slot_index[0]
    target = slot_here // vis_dev
    slot_lane = slot_here % run_length
    local_row = slot_here % vis_dev
    send_place = jnp.where(kept_here, target * run_length + slot_lane, seq_count * run_length)
    outgoing = (
        jnp.zeros((seq_count * run_length, D), jnp.bfloat16)
        .at[send_place]
        .set(embedded, mode="drop")
    )
    labels = (
        jnp.full((seq_count * run_length,), vis_dev, jnp.int32)
        .at[send_place]
        .set(local_row, mode="drop")
    )
    arrived, arrived_rows = (
        lax.all_to_all(
            outgoing.reshape(seq_count, run_length, D),
            "seq",
            split_axis=0,
            concat_axis=0,
            tiled=True,
        ),
        lax.all_to_all(
            labels.reshape(seq_count, run_length), "seq", split_axis=0, concat_axis=0, tiled=True
        ),
    )
    arrived = arrived.reshape(seq_count * run_length, D)
    arrived_rows = arrived_rows.reshape(seq_count * run_length)
    visible = jnp.zeros((vis_dev, D), jnp.bfloat16).at[arrived_rows].set(arrived, mode="drop")
    normed = layer_norm(visible.astype(jnp.float32)).astype(jnp.bfloat16)
    group_w = qkv_proj.shape[3]
    projected = jnp.dot(
        normed, qkv_proj.reshape(D, 3 * group_w), preferred_element_type=jnp.float32
    ).astype(jnp.bfloat16)
    queries = projected[:, :group_w]
    pairs_here = projected[:, group_w:]
    pairs_prev = passed_along(pairs_here, "seq", 1)
    attended = attend_block(queries, pairs_here, pairs_prev, group_w)
    rows_owned = lax.dynamic_slice_in_dim(out_proj, pair_here * group_w, group_w, 0)
    head_mixed = lax.psum(
        jnp.dot(attended, rows_owned, preferred_element_type=jnp.float32).astype(jnp.bfloat16),
        "canvas",
    ).astype(jnp.float32)
    residual = visible.astype(jnp.float32) + head_mixed
    normed_two = layer_norm(residual).astype(jnp.bfloat16)
    up_full = lax.all_gather(up_proj, "fsdp", axis=0, tiled=True)
    hidden = jax.nn.gelu(
        jnp.dot(normed_two, up_full, preferred_element_type=jnp.float32), approximate=False
    ).astype(jnp.bfloat16)
    output_terms = lax.dot_general(
        hidden,
        lax.all_gather(down_proj, "fsdp", axis=0, tiled=True),
        (((1,), (1,)), ((), ())),
        preferred_element_type=jnp.float32,
    )
    row_share = lax.psum_scatter(
        output_terms.astype(jnp.bfloat16), "canvas", scatter_dimension=0, tiled=True
    ).astype(jnp.float32)
    share_count = row_share.shape[0]
    base_rows = lax.dynamic_slice_in_dim(residual, pair_here * share_count, share_count, 0)
    return (base_rows + row_share).astype(jnp.bfloat16)[None]


def solution(mesh):
    placed = (
        P("fsdp", "seq", None),
        P("fsdp", "seq"),
        P("fsdp", "seq"),
        P("fsdp", "seq"),
        P(None, "canvas", None, None),
        P(),
        P("fsdp", "canvas"),
        P("fsdp", "canvas"),
    )
    return jax.shard_map(
        shards,
        mesh=mesh,
        in_specs=placed,
        out_specs=P("fsdp", ("seq", "canvas"), None),
        check_vma=False,
    )
```

profile of v0, /device:TPU:1, one launch (start us, length us, event | category | flops | bytes accessed | tf_op | source)
XLA Modules:
  0.0 243.6 jit_solution(1902748353965721082)
XLA Ops:
  7.4 0.9 compare_select_fusion.1
  8.9 1.4 scatter_custom_fusion
  11.0 25.6 %all-to-all-start = ((s32[64,1,4]{2,1,0:T(1,128)}), s32[64,1,4]{2,1,0:T(1,128)S(1)}, u32[]{:S(2)}, u32[]{:S(2)}) async-start(s32[64,1,4]{2,1,0:T(1,128)} %bitcast.4), calls=%async_computation | async-start | bytes 65536 | tf_op jit(solution)/shard_map/all_to_all | solution.py:95
  36.6 0.7 broadcast_in_dim.15
  37.5 2.7 %multiply_sine_fusion.1 = (f32[256,256]{1,0:T(8,128)S(1)}, f32[256,256]{1,0:T(8,128)S(1)}, f32[256,256]{1,0:T(8,128)S(1)}, f32[256,256]{1,0:T(8,128)}) fusion(f32[256]{0:T(256)S(1)} %multiply_power_fusion, f32[256]{0:T(256)S(1)} %get-tuple-element.15, f32[256]{0:T(256)S(1)} %get-tuple-element.16), kind=kLoop, calls=%fused_computation.82 | loop fusion | flops 131072 | bytes 1051648 | tf_op jit(solution)/shard_map/sin | solution.py:39
  40.2 2.5 %scatter_custom_fusion.1 = bf16[256,1024]{1,0:T(8,128)(2,1)S(1)} fusion(s32[256]{0:T(256)S(1)} %bitcast.57, f32[256,256]{1,0:T(8,128)S(1)} %get-tuple-element.13, f32[]{:T(128)} %constant.150.clone.1, f32[256,256]{1,0:T(8,128)} %get-tuple-element.14, f32[256,256]{1,0:T(8,128)S(1)} %get-tuple-element.10, f32[256,256]{1,0:T(8,128)S(1)} %get-tuple-element.9, ...), kind=kCustom, calls=%fused_computation.42 | custom fusion | flops 1572864 | bytes 2097158 | tf_op jit(solution)/shard_map/scatter | solution.py:80
  42.7 1.0 reshape.321
  43.6 8.8 %all-to-all-done = s32[64,1,4]{2,1,0:T(1,128)S(1)} async-done(((s32[64,1,4]{2,1,0:T(1,128)}), s32[64,1,4]{2,1,0:T(1,128)S(1)}, u32[]{:S(2)}, u32[]{:S(2)}) %all-to-all-start) | async-done | bytes 1056 | tf_op jit(solution)/shard_map/all_to_all | solution.py:95
  52.4 8.2 %all-to-all-start.1 = ((bf16[64,4,1024]{2,1,0:T(4,128)(2,1)}), bf16[64,4,1024]{2,1,0:T(4,128)(2,1)S(1)}, u32[]{:S(2)}, u32[]{:S(2)}) async-start(bf16[64,4,1024]{2,1,0:T(4,128)(2,1)} %reshape.321), calls=%async_computation.1 | async-start | bytes 1048576 | tf_op jit(solution)/shard_map/all_to_all | solution.py:88
  60.6 4.7 %copy.17 = bf16[1024,1,3,512]{0,3,2,1:T(8,128)(2,1)} copy(bf16[1024,1,3,512]{3,0,2,1:T(8,128)(2,1)} %param.12) | data formatting | bytes 6291456 | tf_op args[4]
  65.8 0.7 reduce.3
  66.7 24.2 %all-to-all-done.1 = bf16[64,4,1024]{2,1,0:T(4,128)(2,1)S(1)} async-done(((bf16[64,4,1024]{2,1,0:T(4,128)(2,1)}), bf16[64,4,1024]{2,1,0:T(4,128)(2,1)S(1)}, u32[]{:S(2)}, u32[]{:S(2)}) %all-to-all-start.1) | async-done | bytes 524320 | tf_op jit(solution)/shard_map/all_to_all | solution.py:88
  91.0 1.7 scatter_custom_fusion.2
  93.1 3.1 %convolution_convert_fusion = bf16[128,1536]{1,0:T(8,128)(2,1)S(1)} fusion(bf16[1024,1536]{0,1:T(8,128)(2,1)} %bitcast.49, bf16[128,1024]{1,0:T(8,128)(2,1)S(1)} %scatter_custom_fusion.2, f32[128]{0:T(128)S(1)} %add_rsqrt_fusion.1, f32[128]{0:T(128)S(1)} %broadcast_multiply_fusion.1), kind=kOutput, calls=%fused_computation.3 | convolution fusion | flops 403374080 | bytes 3802112 | tf_op jit(solution)/shard_map/dot_general | solution.py:104
  96.2 4.4 %collective-permute-start = (bf16[128,1024]{1,0:T(8,128)(2,1)S(1)}, bf16[128,1024]{1,0:T(8,128)(2,1)S(1)}, u32[]{:S(2)}, u32[]{:S(2)}) collective-permute-start(bf16[128,1024]{1,0:T(8,128)(2,1)S(1)} %slice.16), channel_id=1, source_target_pairs={{0,16},{16,32},{32,48},{48,64},{64,80},{80,96},{96,112},{112,128},... | collective-permute-start | bytes 786440 | tf_op jit(solution)/shard_map/ppermute | solution.py:18
  100.7 8.8 %collective-permute-done = bf16[128,1024]{1,0:T(8,128)(2,1)S(1)} collective-permute-done((bf16[128,1024]{1,0:T(8,128)(2,1)S(1)}, bf16[128,1024]{1,0:T(8,128)(2,1)S(1)}, u32[]{:S(2)}, u32[]{:S(2)}) %collective-permute-start) | collective-permute-done | bytes 262176 | tf_op jit(solution)/shard_map/ppermute | solution.py:18
  111.1 1.0 convolution_convert_fusion.1
  113.6 45.6 %all-reduce.2.cloned.1.call-done = bf16[128,1024]{1,0:T(8,128)(2,1)} async-done(((bf16[128,1024]{1,0:T(8,128)(2,1)}), bf16[128,1024]{1,0:T(8,128)(2,1)}) %all-reduce.2.cloned.1.call-update) | async-done | bytes 262160 | tf_op jit(solution)/shard_map/psum | solution.py:112
  159.2 1.1 convert_add_fusion
  160.3 1.2 multiply_reduce_fusion
  161.5 39.7 %all-gather.5.cloned.1.call-done = bf16[1024,2048]{1,0:T(8,128)(2,1)} async-done(((bf16[128,2048]{1,0:T(8,128)(2,1)}), bf16[1024,2048]{1,0:T(8,128)(2,1)}) %all-gather.5.cloned.1.call-update) | async-done | bytes 4194320 | tf_op jit(solution)/shard_map/all_gather | solution.py:124
  201.1 8.6 %convolution_convert_fusion.2 = bf16[128,1024]{1,0:T(8,128)(2,1)} fusion(bf16[1024,2048]{1,0:T(8,128)(2,1)} %all-gather.5.cloned.1.call-done, bf16[1024,2048]{1,0:T(8,128)(2,1)} %all-gather.3.cloned.1.call-done, f32[128]{0:T(128)S(1)} %add_rsqrt_fusion, f32[128]{0:T(128)S(1)} %broadcast_multiply_fusion, bf16[128,1024]{1,0:T(8,128)(2,1)S(1)} %scatter_custom_fusion.2, ...), kind=kOutput, calls=%fused_computation.7 | convolution fusion | flops 1091698688 | bytes 9176064 | tf_op jit(solution)/shard_map/dot_general | solution.py:122
  209.7 24.8 %reduce-scatter.2.cloned.1.call-done = bf16[64,1024]{1,0:T(8,128)(2,1)} async-done(((bf16[128,1024]{1,0:T(8,128)(2,1)}), bf16[64,1024]{1,0:T(8,128)(2,1)}) %reduce-scatter.2.cloned.1.call-update) | async-done | bytes 131088 | tf_op jit(solution)/shard_map/reduce_scatter | solution.py:128
  234.6 1.6 fusion.66
  (35 shorter events, 5.7 us)
Async XLA Ops:
  7.4 103.7 %copy-start = (bf16[1024,1024]{1,0:T(8,128)(2,1)S(1)}, bf16[1024,1024]{1,0:T(8,128)(2,1)}, u32[]{:S(2)}) copy-start(bf16[1024,1024]{1,0:T(8,128)(2,1)} %param.13) | copy-start | bytes 6291460
  11.0 41.4 %all-to-all-start = ((s32[64,1,4]{2,1,0:T(1,128)}), s32[64,1,4]{2,1,0:T(1,128)S(1)}, u32[]{:S(2)}, u32[]{:S(2)}) async-start(s32[64,1,4]{2,1,0:T(1,128)} %bitcast.4), calls=%async_computation | async-start | bytes 65536 | tf_op jit(solution)/shard_map/all_to_all | solution.py:95
  52.4 38.5 %all-to-all-start.1 = ((bf16[64,4,1024]{2,1,0:T(4,128)(2,1)}), bf16[64,4,1024]{2,1,0:T(4,128)(2,1)S(1)}, u32[]{:S(2)}, u32[]{:S(2)}) async-start(bf16[64,4,1024]{2,1,0:T(4,128)(2,1)} %reshape.321), calls=%async_computation.1 | async-start | bytes 1048576 | tf_op jit(solution)/shard_map/all_to_all | solution.py:88
  60.6 98.6 %all-reduce.2.cloned.1.call-start = ((), (), s32[]{:S(2)}) async-start(), calls=%async_computation.3 | async-start | bytes 524288 | tf_op jit(solution)/shard_map/psum | solution.py:112
  96.2 13.4 %collective-permute-start = (bf16[128,1024]{1,0:T(8,128)(2,1)S(1)}, bf16[128,1024]{1,0:T(8,128)(2,1)S(1)}, u32[]{:S(2)}, u32[]{:S(2)}) collective-permute-start(bf16[128,1024]{1,0:T(8,128)(2,1)S(1)} %slice.16), channel_id=1, source_target_pairs={{0,16},{16,32},{32,48},{48,64},{64,80},{80,96},{96,112},{112,128},... | collective-permute-start | bytes 786440 | tf_op jit(solution)/shard_map/ppermute | solution.py:18
  112.2 49.3 %all-gather.3.cloned.1.call-start = ((), (), s32[]{:S(2)}) async-start(), calls=%async_computation.4 | async-start | bytes 4718592 | tf_op jit(solution)/shard_map/all_gather | solution.py:118
  112.7 88.4 %all-gather.5.cloned.1.call-start = ((), (), s32[]{:S(2)}) async-start(), calls=%async_computation.5 | async-start | bytes 4718592 | tf_op jit(solution)/shard_map/all_gather | solution.py:124
  113.3 121.2 %reduce-scatter.2.cloned.1.call-start = ((), (), s32[]{:S(2)}) async-start(), calls=%async_computation.6 | async-start | bytes 393216 | tf_op jit(solution)/shard_map/reduce_scatter | solution.py:128
Sparse Core Ops, SparseCore 0:
  112.3 46.8 all-reduce.1
  209.9 24.6 reduce-scatter.1
Sparse Core Ops, SparseCore 1:
  115.7 39.5 all-gather.2
  158.3 42.8 all-gather.4
where the time goes:
time: 244 us
  waiting for transfers between devices  153 us (63%)
  starting transfers between devices  38.5 us (16%)
  between operations  15 us (6%)
  matrix products  13.5 us (6%)
  other arithmetic  12.1 us (5%)
  local copies, waits for them, and re-layouts  11.4 us (5%)
    psum x1, waiting for transfers between devices, shards(): lax.psum(jnp.dot(attended, rows_owned, preferred_element_type=jnp.float32...  45.6 us
    all_gather x1, waiting for transfers between devices, shards(): lax.all_gather(down_proj, 'fsdp', axis=0, tiled=True)  39.7 us
    all_to_all x1, starting transfers between devices, shards(): lax.all_to_all(labels.reshape(seq_count, run_length), 'seq', split_axis=0...  25.6 us
    reduce_scatter x1, waiting for transfers between devices, shards(): lax.psum_scatter(output_terms.astype(jnp.bfloat16), 'canvas', scatter_dim...  24.8 us
    all_to_all x1, waiting for transfers between devices, shards(): lax.all_to_all(outgoing.reshape(seq_count, run_length, D), 'seq', split_a...  24.2 us
    ppermute x1, waiting for transfers between devices, passed_along(): return lax.ppermute(value, axis, pairs)  8.84 us
    all_to_all x1, waiting for transfers between devices, shards(): lax.all_to_all(labels.reshape(seq_count, run_length), 'seq', split_axis=0...  8.77 us
    dot_general x1, matrix products, shards(): lax.dot_general(hidden, lax.all_gather(down_proj, 'fsdp', axis=0, tiled=T...  8.58 us
  transfers between devices with their start and end apart: 7, of which 6 were waited for; matrix products, arithmetic and copies ran while one was open for 6% of the time, Pallas kernels for 0%

commit v1 on v0

v1 whole, which is shorter than its diff:
```python
import functools

import jax
import jax.numpy as jnp
import numpy as np
from jax import lax
from jax.experimental import pallas as pl
from jax.experimental.pallas import tpu as pltpu
from jax.sharding import PartitionSpec as P

D = 1024
HALF = 512
QUART = 256
EPS = 1e-06
MESH = pl.DeviceIdType.MESH
F32 = jnp.float32
BF16 = jnp.bfloat16


def normalised(values):
    centered = values - jnp.mean(values, axis=-1, keepdims=True)
    spread = jnp.mean(centered * centered, axis=-1, keepdims=True)
    return centered * lax.rsqrt(spread + EPS)


def matmul(left, right):
    return jnp.dot(left, right, preferred_element_type=F32)


def matmul_nt(left, right):
    return lax.dot_general(left, right, (((1,), (1,)), ((), ())), preferred_element_type=F32)


def gelu(x):
    return 0.5 * x * (1.0 + lax.erf(x * (0.5**0.5)))


def kernel(
    n_seq, chunks,
    tile_ref, keep_ref, slot_ref, freq_ref, patch_hbm, qkv_hbm, out_hbm, up_hbm, down_hbm,
    y_ref,
    patch_v, qkv_v, out_v, up_v, down_v,
    emb, send, recv, lab_out, lab_in, vis, normed, q_s, k_s, v_s, att, resid, normed2, hidden, part, y_out, y_in,
    load_sem, a2a_sem, vis_ssem, vis_rsem, w_ssem, w_rsem, att_sem, y_ssem, y_rsem,
):
    s = lax.axis_index("seq")
    f = lax.axis_index("fsdp")
    c = lax.axis_index("canvas")
    other = 1 - c
    f_right, f_left, f_far = lax.rem(f + 2, 8), lax.rem(f + 6, 8), lax.rem(f + 4, 8)
    mate = f + 1 - 2 * lax.rem(f, 2)
    m_right, m_left, m_far = lax.rem(mate + 2, 8), lax.rem(mate + 6, 8), lax.rem(mate + 4, 8)
    s_next = lax.rem(s + 1, n_seq)
    s_diag = lax.rem(s + n_seq + 2 * c - 1, n_seq)

    barrier = pltpu.get_barrier_semaphore()

    def greet(i, carry):
        pl.semaphore_signal(barrier, inc=1, device_id={"seq": lax.rem(s + i, n_seq)}, device_id_type=MESH)
        return carry

    lax.fori_loop(1, n_seq, greet, 0)
    for peer in (f_right, f_left, mate):
        pl.semaphore_signal(barrier, inc=1, device_id={"fsdp": peer}, device_id_type=MESH)
    pl.semaphore_signal(barrier, inc=1, device_id={"canvas": other}, device_id_type=MESH)
    pl.semaphore_signal(barrier, inc=1, device_id={"seq": s_diag, "canvas": other}, device_id_type=MESH)

    col0 = pl.multiple_of(c * HALF, HALF)
    patch_load = pltpu.make_async_copy(patch_hbm.at[0, :, pl.ds(col0, HALF)], patch_v, load_sem.at[0])
    qkv_load = pltpu.make_async_copy(qkv_hbm, qkv_v, load_sem.at[1])
    out_load = pltpu.make_async_copy(out_hbm, out_v, load_sem.at[2])

    def rows_of(shard):
        return pl.ds(pl.multiple_of(shard * 128, 128), 128)

    up_load = pltpu.make_async_copy(up_hbm, up_v.at[rows_of(f)], load_sem.at[3])
    down_load = pltpu.make_async_copy(down_hbm, down_v.at[rows_of(f)], load_sem.at[4])
    for load in (patch_load, qkv_load, out_load, up_load, down_load):
        load.start()

    slot = slot_ref[...]
    kept = keep_ref[...] == 1
    target = slot // 128
    lane4 = lax.rem(slot, 4)
    group = lax.rem(slot, 128) // 4
    first = jnp.where(kept & (lane4 == 0), target, -1)
    group_val = jnp.broadcast_to((group + 1).astype(F32), (8, 256)).astype(BF16)
    t_rows = lax.broadcasted_iota(jnp.int32, (128, 256), 0)
    hit = jnp.where(t_rows == first, 1.0, 0.0).astype(BF16)
    labels = matmul_nt(group_val, hit)
    lab_out[...] = labels[0:1, :]

    patch_load.wait()
    freq = freq_ref[...]
    within = lax.broadcasted_iota(jnp.int32, (16, QUART), 0)
    cell = jnp.where(c == 0, within // 4, lax.rem(within, 4))

    def embed(t, carry):
        tile = tile_ref[0, t]
        base = jnp.where(c == 0, tile // 32, lax.rem(tile, 32)) * 4
        angle = (base + cell).astype(F32) * freq
        rows = pl.ds(pl.multiple_of(t * 16, 16), 16)
        emb[0, rows, :] = (patch_v[rows, 0:QUART].astype(F32) + jnp.sin(angle)).astype(BF16)
        emb[1, rows, :] = (patch_v[rows, QUART:HALF].astype(F32) + jnp.cos(angle)).astype(BF16)
        return carry

    lax.fori_loop(0, 16, embed, 0)

    key = jnp.where(kept, target * 4 + lane4, -1000)
    row_i = lax.broadcasted_iota(jnp.int32, (512, QUART), 0)
    row_key = row_i // 8 * 4 + lax.rem(row_i, 4) + lax.rem(row_i // 4, 2) * 256
    pick0 = jnp.where(row_key == key, 1.0, 0.0).astype(BF16)
    pick1 = jnp.where(row_key == key + 256, 1.0, 0.0).astype(BF16)
    packed = matmul(pick0, emb[0]) + matmul(pick1, emb[1])
    send[...] = packed.astype(BF16).reshape(n_seq, 8, QUART)

    pl.semaphore_wait(barrier, n_seq + 4)

    def push(i, carry):
        step = 32 + (i + 1) // 2 * (2 * lax.rem(i, 2) - 1)
        to = lax.rem(s + step, n_seq)
        pltpu.make_async_remote_copy(
            src_ref=lab_out, dst_ref=lab_in.at[s], send_sem=a2a_sem.at[0], recv_sem=a2a_sem.at[1],
            device_id={"seq": to}, device_id_type=MESH,
        ).start()
        pltpu.make_async_remote_copy(
            src_ref=send.at[to], dst_ref=recv.at[s], send_sem=a2a_sem.at[2], recv_sem=a2a_sem.at[3],
            device_id={"seq": to}, device_id_type=MESH,
        ).start()
        return carry

    lax.fori_loop(0, n_seq - 1, push, 0)
    own_label = pltpu.make_async_copy(lab_out, lab_in.at[s], a2a_sem.at[4])
    own_label.start()
    own_rows = pltpu.make_async_copy(send.at[s], recv.at[s], a2a_sem.at[5])
    own_rows.start()

    def ship(src, buf, shard, to, index_s, index_r):
        copy = pltpu.make_async_remote_copy(
            src_ref=src, dst_ref=buf.at[rows_of(shard)], send_sem=w_ssem.at[index_s], recv_sem=w_rsem.at[index_r],
            device_id={"fsdp": to}, device_id_type=MESH,
        )
        copy.start()
        return copy

    def landed(buf, shard, index_r):
        view = buf.at[rows_of(shard)]
        pltpu.make_async_copy(view, view, w_rsem.at[index_r]).wait()

    shipped = [
        ship(up_hbm, up_v, f, f_right, 0, 0),
        ship(down_hbm, down_v, f, f_left, 1, 3),
        ship(down_hbm, down_v, f, f_right, 2, 1),
        ship(up_hbm, up_v, f, f_left, 3, 2),
        ship(up_hbm, up_v, f, mate, 4, 6),
        ship(down_hbm, down_v, f, mate, 5, 7),
    ]

    own_label.wait()
    pltpu.make_async_copy(lab_in.at[pl.ds(0, n_seq - 1)], lab_in.at[pl.ds(0, n_seq - 1)], a2a_sem.at[1]).wait()
    lane_of = lax.broadcasted_iota(jnp.int32, (8, 128), 1)
    mine = jnp.where(lane_of == s, 1.0, 0.0).astype(BF16)
    came = matmul_nt(mine, lab_in[...].reshape(n_seq, 128).astype(BF16))
    spread_r = lax.broadcasted_iota(jnp.int32, (n_seq, 512), 0)
    spread_c = lax.broadcasted_iota(jnp.int32, (n_seq, 512), 1)
    spread = jnp.where(spread_r == spread_c // 8, 1.0, 0.0).astype(BF16)
    label_of = matmul(came.astype(BF16), spread).astype(jnp.int32)
    col_i = lax.broadcasted_iota(jnp.int32, (8, 512), 1)
    row_of = label_of * 4 - 4 + lax.rem(col_i, 4)
    half_of = lax.rem(col_i // 4, 2)
    r_i = lax.broadcasted_iota(jnp.int32, (128, 512), 0)
    places = []
    for h in range(2):
        row_h = jnp.where(half_of == h, row_of, -1)[0:1, :]
        places.append(jnp.where(r_i == row_h, 1.0, 0.0).astype(BF16))
    own_rows.wait()
    pltpu.make_async_copy(recv.at[pl.ds(0, n_seq - 1)], recv.at[pl.ds(0, n_seq - 1)], a2a_sem.at[3]).wait()
    came_rows = recv[...].reshape(512, QUART)
    for h in range(2):
        vis[0, c, :, h * QUART:(h + 1) * QUART] = matmul(places[h], came_rows).astype(BF16)

    size = 128 // chunks

    def view_of(block, half, k):
        return vis.at[block, half, pl.ds(k * size, size), :]

    def pass_on(half, src_block, dst_block, k, to, index_s, index_r):
        copy = pltpu.make_async_remote_copy(
            src_ref=view_of(src_block, half, k), dst_ref=view_of(dst_block, half, k),
            send_sem=vis_ssem.at[index_s * chunks + k], recv_sem=vis_rsem.at[index_r * chunks + k],
            device_id=to, device_id_type=MESH,
        )
        copy.start()
        return copy

    def arrived(block, half, k, index_r):
        view = view_of(block, half, k)
        pltpu.make_async_copy(view, view, vis_rsem.at[index_r * chunks + k]).wait()

    def sent(half, k, index_s):
        view = view_of(0, half, k)
        pltpu.make_async_copy(view, view, vis_ssem.at[index_s * chunks + k]).wait()

    pair = {"canvas": other}
    onward = {"seq": s_next, "canvas": 0}
    for k in range(chunks):
        pass_on(c, 0, 0, k, pair, 0, 0)

    @pl.when(c == 1)
    def _():
        for k in range(chunks):
            pass_on(1, 0, 1, k, onward, 1, 1)
        for k in range(chunks):
            arrived(0, 0, k, 0)
            pass_on(0, 0, 1, k, onward, 2, 2)

    @pl.when(c == 0)
    def _():
        for k in range(chunks):
            arrived(1, 1, k, 1)
            pass_on(1, 1, 1, k, pair, 1, 1)
        for k in range(chunks):
            arrived(0, 1, k, 0)

    landed(up_v, f_left, 0)
    shipped.append(ship(up_v.at[rows_of(f_left)], up_v, f_left, f_right, 6, 4))
    landed(down_v, f_right, 3)
    shipped.append(ship(down_v.at[rows_of(f_right)], down_v, f_right, f_left, 7, 5))
    shipped.append(ship(up_v.at[rows_of(f_left)], up_v, f_left, mate, 8, 8))
    shipped.append(ship(down_v.at[rows_of(f_right)], down_v, f_right, mate, 9, 11))

    qkv_load.wait()
    visible = jnp.concatenate([vis[0, 0], vis[0, 1]], axis=1).astype(F32)
    normed[...] = normalised(visible).astype(BF16)
    q_s[...] = matmul(normed[...], qkv_v[0]).astype(BF16)
    k_s[0:128, :] = matmul(normed[...], qkv_v[1]).astype(BF16)
    v_s[0:128, :] = matmul(normed[...], qkv_v[2]).astype(BF16)

    @pl.when(c == 0)
    def _():
        for k in range(chunks):
            arrived(1, 0, k, 2)
            pass_on(0, 1, 1, k, pair, 2, 2)

    @pl.when(c == 1)
    def _():
        for k in range(chunks):
            arrived(1, 1, k, 1)
        for k in range(chunks):
            arrived(1, 0, k, 2)

    before = jnp.concatenate([vis[1, 0], vis[1, 1]], axis=1).astype(F32)
    normed[...] = normalised(before).astype(BF16)
    k_s[128:256, :] = matmul(normed[...], qkv_v[1]).astype(BF16)
    v_s[128:256, :] = matmul(normed[...], qkv_v[2]).astype(BF16)

    low = lax.broadcasted_iota(jnp.int32, (128, 128), 1) < 64
    for p in range(4):
        lanes = pl.ds(p * 128, 128)
        q_pair, k_pair, v_pair = q_s[:, lanes], k_s[:, lanes], v_s[:, lanes]
        mixed = []
        for e in range(2):
            q_one = jnp.where(low == (e == 0), q_pair.astype(F32), 0.0).astype(BF16)
            scores = matmul_nt(q_one, k_pair) * 0.125
            expo = jnp.exp(scores - jnp.max(scores, axis=-1, keepdims=True))
            total = jnp.sum(expo, axis=-1, keepdims=True)
            mixed.append(matmul(expo.astype(BF16), v_pair) / total)
        att[c, :, lanes] = jnp.where(low, mixed[0], mixed[1]).astype(BF16)

    att_copy = pltpu.make_async_remote_copy(
        src_ref=att.at[c], dst_ref=att.at[c], send_sem=att_sem.at[0], recv_sem=att_sem.at[1],
        device_id=pair, device_id_type=MESH,
    )
    att_copy.start()

    landed(down_v, f_left, 1)
    shipped.append(ship(down_v.at[rows_of(f_left)], down_v, f_left, mate, 10, 9))
    landed(up_v, f_right, 2)
    shipped.append(ship(up_v.at[rows_of(f_right)], up_v, f_right, mate, 11, 10))

    out_load.wait()
    att_copy.wait_recv()
    mixed_in = jnp.concatenate([att[0], att[1]], axis=1)
    visible = jnp.concatenate([vis[0, 0], vis[0, 1]], axis=1).astype(F32)
    resid[...] = visible + matmul(mixed_in, out_v[...])
    normed2[...] = normalised(resid[...]).astype(BF16)

    landed(up_v, f_far, 4)
    shipped.append(ship(up_v.at[rows_of(f_far)], up_v, f_far, mate, 12, 12))
    landed(down_v, f_far, 5)
    shipped.append(ship(down_v.at[rows_of(f_far)], down_v, f_far, mate, 13, 13))

    up_load.wait()
    down_load.wait()
    landed(up_v, mate, 6)
    landed(up_v, m_left, 8)
    landed(up_v, m_right, 10)
    landed(up_v, m_far, 12)

    def widen(n, carry):
        cols = pl.ds(pl.multiple_of(n * 256, 256), 256)
        hidden[:, cols] = gelu(matmul(normed2[...], up_v[:, cols])).astype(BF16)
        return carry

    lax.fori_loop(0, 8, widen, 0)

    landed(down_v, mate, 7)
    landed(down_v, m_left, 9)
    landed(down_v, m_right, 11)
    landed(down_v, m_far, 13)

    here = pl.ds(pl.multiple_of(c * 64, 64), 64)
    there = pl.ds(pl.multiple_of(other * 64, 64), 64)
    y_copies = []
    for n in range(4):
        cols = pl.ds(n * 256, 256)
        part[:, cols] = matmul_nt(hidden[...], down_v[n * 256:(n + 1) * 256, :])
        y_out[n] = part[there, cols].astype(BF16)
        copy = pltpu.make_async_remote_copy(
            src_ref=y_out.at[n], dst_ref=y_in.at[n], send_sem=y_ssem.at[n], recv_sem=y_rsem.at[n],
            device_id=pair, device_id_type=MESH,
        )
        copy.start()
        y_copies.append(copy)
    for n in range(4):
        cols = pl.ds(n * 256, 256)
        y_copies[n].wait_recv()
        y_ref[:, cols] = (resid[here, cols] + part[here, cols] + y_in[n].astype(F32)).astype(BF16)

    first63 = pl.ds(0, n_seq - 1)
    pltpu.make_async_copy(lab_in.at[first63], lab_in.at[first63], a2a_sem.at[0]).wait()
    pltpu.make_async_copy(send.at[first63], send.at[first63], a2a_sem.at[2]).wait()
    for index_s in range(3):
        for k in range(chunks):
            sent(0, k, index_s)
    for copy in shipped:
        copy.wait_send()
    att_copy.wait_send()
    for copy in y_copies:
        copy.wait_send()


def shards(chunks, patch_tokens, keep_mask, slot_index, tile_map, qkv_proj, out_proj, up_proj, down_proj):
    n_seq = lax.axis_size("seq")
    freq = jnp.asarray((10000.0 ** (-np.arange(QUART) / QUART)).astype(np.float32)).reshape(1, QUART)
    qkv = jnp.transpose(qkv_proj, (1, 2, 0, 3)).reshape(3, D, HALF)
    hbm = pl.BlockSpec(memory_space=pl.ANY)
    vmem = pl.BlockSpec(memory_space=pltpu.VMEM)
    y = pl.pallas_call(
        functools.partial(kernel, n_seq, chunks),
        name="encoder_layer",
        out_shape=jax.ShapeDtypeStruct((64, D), BF16),
        in_specs=[pl.BlockSpec(memory_space=pltpu.SMEM), vmem, vmem, vmem, hbm, hbm, hbm, hbm, hbm],
        out_specs=vmem,
        scratch_shapes=[
            pltpu.VMEM((256, HALF), BF16),
            pltpu.VMEM((3, D, HALF), BF16),
            pltpu.VMEM((D, D), BF16),
            pltpu.VMEM((D, 2048), BF16),
            pltpu.VMEM((D, 2048), BF16),
            pltpu.VMEM((2, 256, QUART), BF16),
            pltpu.VMEM((n_seq, 8, QUART), BF16),
            pltpu.VMEM((n_seq, 8, QUART), BF16),
            pltpu.VMEM((1, 128), F32),
            pltpu.VMEM((n_seq, 1, 128), F32),
            pltpu.VMEM((2, 2, 128, HALF), BF16),
            pltpu.VMEM((128, D), BF16),
            pltpu.VMEM((128, HALF), BF16),
            pltpu.VMEM((256, HALF), BF16),
            pltpu.VMEM((256, HALF), BF16),
            pltpu.VMEM((2, 128, HALF), BF16),
            pltpu.VMEM((128, D), F32),
            pltpu.VMEM((128, D), BF16),
            pltpu.VMEM((128, 2048), BF16),
            pltpu.VMEM((128, D), F32),
            pltpu.VMEM((4, 64, 256), BF16),
            pltpu.VMEM((4, 64, 256), BF16),
            pltpu.SemaphoreType.DMA((5,)),
            pltpu.SemaphoreType.DMA((6,)),
            pltpu.SemaphoreType.DMA((3 * chunks,)),
            pltpu.SemaphoreType.DMA((3 * chunks,)),
            pltpu.SemaphoreType.DMA((14,)),
            pltpu.SemaphoreType.DMA((14,)),
            pltpu.SemaphoreType.DMA((2,)),
            pltpu.SemaphoreType.DMA((4,)),
            pltpu.SemaphoreType.DMA((4,)),
        ],
        compiler_params=pltpu.CompilerParams(
            collective_id=0, has_side_effects=True, vmem_limit_bytes=50 * 1024 * 1024
        ),
    )(tile_map, keep_mask, slot_index, freq, patch_tokens, qkv, out_proj, up_proj, down_proj)
    return y[None]


def solution(mesh):
    placed = (
        P("fsdp", "seq", None),
        P("fsdp", "seq"),
        P("fsdp", "seq"),
        P("fsdp", "seq"),
        P(None, "canvas", None, None),
        P(),
        P("fsdp", "canvas"),
        P("fsdp", "canvas"),
    )
    return jax.shard_map(
        functools.partial(shards, 2),
        mesh=mesh,
        in_specs=placed,
        out_specs=P("fsdp", ("seq", "canvas"), None),
        check_vma=False,
    )
```

time: 244 us -> 81.6 us (0.33)
  waiting for transfers between devices: 153 us -> 0 us
  Pallas kernels: 0 us -> 73.2 us
  starting transfers between devices: 38.5 us -> 0 us
  between operations: 15 us -> 0.02 us
  matrix products: 13.5 us -> 0 us
  other arithmetic: 12.1 us -> 0 us
  local copies, waits for them, and re-layouts: 11.4 us -> 8.06 us
    pallas_call x0 -> x1, Pallas kernels: none -> 73.2 us  [shards(): pl.pallas_call(functools.partial(kernel, n_seq, chunks), name='encoder_la...]
    psum x1 -> x0, waiting for transfers between devices: 45.6 us -> none  [shards(): lax.psum(jnp.dot(attended, rows_owned, preferred_element_type=jnp.float32...]
    all_gather x2 -> x0, waiting for transfers between devices: 39.7 us -> none  [the longest x1 39.7 us: shards(): lax.all_gather(down_proj, 'fsdp', axis=0, tiled=True)]
    all_to_all x2 -> x0, starting transfers between devices: 33.7 us -> none  [the longest x1 25.6 us: shards(): lax.all_to_all(labels.reshape(seq_count, run_length), 'seq', split_axis=0...]
    all_to_all x2 -> x0, waiting for transfers between devices: 33 us -> none  [the longest x1 24.2 us: shards(): lax.all_to_all(outgoing.reshape(seq_count, run_length, D), 'seq', split_a...]
    reduce_scatter x1 -> x0, waiting for transfers between devices: 24.8 us -> none  [shards(): lax.psum_scatter(output_terms.astype(jnp.bfloat16), 'canvas', scatter_dim...]
    dot_general x5 -> x0, matrix products: 13.5 us -> none  [the longest x1 8.58 us: shards(): lax.dot_general(hidden, lax.all_gather(down_proj, 'fsdp', axis=0, tiled=T...]
    ppermute x1 -> x0, waiting for transfers between devices: 8.84 us -> none  [passed_along(): return lax.ppermute(value, axis, pairs)]
  transfers between devices with their start and end apart: 7 -> 0, of which waited for: 6 -> 0; matrix products, arithmetic and copies ran while one was open for 6% -> 0% of each run, Pallas kernels for 0% -> 0%
where the time goes in v1:
time: 81.6 us; the launch traced here: 81.2 us
  Pallas kernels  73.2 us (90%)
  local copies, waits for them, and re-layouts  8.06 us (10%)
    pallas_call x1, Pallas kernels, shards(): pl.pallas_call(functools.partial(kernel, n_seq, chunks), name='encoder_la...  73.2 us
    unnamed x17, local copies, waits for them, and re-layouts  8.06 us

profile of v1, /device:TPU:1, one launch (start us, length us, event | category | flops | bytes accessed | tf_op | source)
XLA Modules:
  0.0 81.2 jit_solution(9809140359191160642)
XLA Ops:
  0.0 0.0 copy-start
  0.0 1.6 %copy-done = bf16[1024,1024]{1,0:T(8,128)(2,1)S(1)} copy-done((bf16[1024,1024]{1,0:T(8,128)(2,1)S(1)}, bf16[1024,1024]{1,0:T(8,128)(2,1)}, u32[]{:S(2)}) %copy-start) | copy-done | bytes 2097176
  1.6 0.0 copy-start.1
  1.6 1.0 %copy-done.1 = bf16[1,256,1024]{2,1,0:T(8,128)(2,1)S(1)} copy-done((bf16[1,256,1024]{2,1,0:T(8,128)(2,1)S(1)}, bf16[1,256,1024]{2,1,0:T(8,128)(2,1)}, u32[]{:S(2)}) %copy-start.1) | copy-done | bytes 524312
  2.6 0.0 copy-start.2
  2.6 1.0 %copy-done.2 = bf16[128,2048]{1,0:T(8,128)(2,1)S(1)} copy-done((bf16[128,2048]{1,0:T(8,128)(2,1)S(1)}, bf16[128,2048]{1,0:T(8,128)(2,1)}, u32[]{:S(2)}) %copy-start.2) | copy-done | bytes 524312
  3.7 0.0 copy-start.3
  3.7 1.0 %copy-done.3 = bf16[128,2048]{1,0:T(8,128)(2,1)S(1)} copy-done((bf16[128,2048]{1,0:T(8,128)(2,1)S(1)}, bf16[128,2048]{1,0:T(8,128)(2,1)}, u32[]{:S(2)}) %copy-start.3) | copy-done | bytes 524312
  4.7 0.0 copy-start.4
  4.7 0.7 copy-done.4
  5.4 0.0 copy-start.5
  5.4 0.7 copy-done.5
  6.1 0.0 copy-start.6
  6.1 0.7 copy-done.6
  6.8 0.0 copy-start.7
  6.8 0.7 copy-done.7
  7.4 73.2 %encoder_layer.1 = bf16[64,1024]{1,0:T(8,128)(2,1)S(1)} custom-call(s32[1,16]{1,0:T(1,128)S(1)} %copy-done.7, s32[1,256]{1,0:T(1,128)S(1)} %copy-done.4, s32[1,256]{1,0:T(1,128)S(1)} %copy-done.5, f32[1,256]{1,0:T(1,128)S(1)} %copy-done.6, bf16[1,256,1024]{2,1,0:T(8,128)(2,1)S(1)} %copy-done.1, bf16[3,1024,512]{2,1,0:T(8,128)(2,1)} %bitcast.5, ...), custom_call_target="tpu_custom_call" | custom-call | tf_op jit(solution)/shard_map/encoder_layer/pallas_call | solution.py:349
  80.6 0.7 copy.11
Async XLA Ops:
  0.0 1.6 %copy-start = (bf16[1024,1024]{1,0:T(8,128)(2,1)S(1)}, bf16[1024,1024]{1,0:T(8,128)(2,1)}, u32[]{:S(2)}) copy-start(bf16[1024,1024]{1,0:T(8,128)(2,1)} %out_hbm.1) | copy-start | bytes 6291460
  1.6 1.0 %copy-start.1 = (bf16[1,256,1024]{2,1,0:T(8,128)(2,1)S(1)}, bf16[1,256,1024]{2,1,0:T(8,128)(2,1)}, u32[]{:S(2)}) copy-start(bf16[1,256,1024]{2,1,0:T(8,128)(2,1)} %patch_hbm.1) | copy-start | bytes 1572868
  2.6 1.0 %copy-start.2 = (bf16[128,2048]{1,0:T(8,128)(2,1)S(1)}, bf16[128,2048]{1,0:T(8,128)(2,1)}, u32[]{:S(2)}) copy-start(bf16[128,2048]{1,0:T(8,128)(2,1)} %up_hbm.1) | copy-start | bytes 1572868
  3.7 1.0 %copy-start.3 = (bf16[128,2048]{1,0:T(8,128)(2,1)S(1)}, bf16[128,2048]{1,0:T(8,128)(2,1)}, u32[]{:S(2)}) copy-start(bf16[128,2048]{1,0:T(8,128)(2,1)} %down_hbm.1) | copy-start | bytes 1572868
  4.7 0.7 copy-start.4
  5.4 0.7 copy-start.5
  6.1 0.7 copy-start.6
  6.8 0.7 copy-start.7

commit v2 on v1

--- a/solution.py
+++ b/solution.py
@@ -37,9 +37,9 @@
 
 def kernel(
     n_seq, chunks,
-    tile_ref, keep_ref, slot_ref, freq_ref, patch_hbm, qkv_hbm, out_hbm, up_hbm, down_hbm,
+    tile_hbm, keep_hbm, slot_hbm, freq_hbm, patch_hbm, qkv_hbm, out_hbm, up_hbm, down_hbm,
     y_ref,
-    patch_v, qkv_v, out_v, up_v, down_v,
+    tile_ref, keep_ref, slot_ref, freq_ref, patch_v, qkv_v, out_v, up_v, down_v,
     emb, send, recv, lab_out, lab_in, vis, normed, q_s, k_s, v_s, att, resid, normed2, hidden, part, y_out, y_in,
     load_sem, a2a_sem, vis_ssem, vis_rsem, w_ssem, w_rsem, att_sem, y_ssem, y_rsem,
 ):
@@ -75,9 +75,19 @@
 
     up_load = pltpu.make_async_copy(up_hbm, up_v.at[rows_of(f)], load_sem.at[3])
     down_load = pltpu.make_async_copy(down_hbm, down_v.at[rows_of(f)], load_sem.at[4])
+    index_loads = [
+        pltpu.make_async_copy(keep_hbm, keep_ref, load_sem.at[5]),
+        pltpu.make_async_copy(slot_hbm, slot_ref, load_sem.at[6]),
+        pltpu.make_async_copy(freq_hbm, freq_ref, load_sem.at[7]),
+        pltpu.make_async_copy(tile_hbm, tile_ref, load_sem.at[8]),
+    ]
+    for load in index_loads:
+        load.start()
     for load in (patch_load, qkv_load, out_load, up_load, down_load):
         load.start()
 
+    for load in index_loads:
+        load.wait()
     slot = slot_ref[...]
     kept = keep_ref[...] == 1
     target = slot // 128
@@ -344,15 +354,19 @@
     n_seq = lax.axis_size("seq")
     freq = jnp.asarray((10000.0 ** (-np.arange(QUART) / QUART)).astype(np.float32)).reshape(1, QUART)
     qkv = jnp.transpose(qkv_proj, (1, 2, 0, 3)).reshape(3, D, HALF)
-    hbm = pl.BlockSpec(memory_space=pl.ANY)
+    hbm = pl.BlockSpec(memory_space=pltpu.HBM)
     vmem = pl.BlockSpec(memory_space=pltpu.VMEM)
     y = pl.pallas_call(
         functools.partial(kernel, n_seq, chunks),
         name="encoder_layer",
         out_shape=jax.ShapeDtypeStruct((64, D), BF16),
-        in_specs=[pl.BlockSpec(memory_space=pltpu.SMEM), vmem, vmem, vmem, hbm, hbm, hbm, hbm, hbm],
+        in_specs=[hbm] * 9,
         out_specs=vmem,
         scratch_shapes=[
+            pltpu.SMEM((1, 16), jnp.int32),
+            pltpu.VMEM((1, 256), jnp.int32),
+            pltpu.VMEM((1, 256), jnp.int32),
+            pltpu.VMEM((1, QUART), F32),
             pltpu.VMEM((256, HALF), BF16),
             pltpu.VMEM((3, D, HALF), BF16),
             pltpu.VMEM((D, D), BF16),
@@ -375,7 +389,7 @@
             pltpu.VMEM((128, D), F32),
             pltpu.VMEM((4, 64, 256), BF16),
             pltpu.VMEM((4, 64, 256), BF16),
-            pltpu.SemaphoreType.DMA((5,)),
+            pltpu.SemaphoreType.DMA((9,)),
             pltpu.SemaphoreType.DMA((6,)),
             pltpu.SemaphoreType.DMA((3 * chunks,)),
             pltpu.SemaphoreType.DMA((3 * chunks,)),
@@ -386,7 +400,7 @@
             pltpu.SemaphoreType.DMA((4,)),
         ],
         compiler_params=pltpu.CompilerParams(
-            collective_id=0, has_side_effects=True, vmem_limit_bytes=50 * 1024 * 1024
+            collective_id=0, has_side_effects=True, vmem_limit_bytes=67043328
         ),
     )(tile_map, keep_mask, slot_index, freq, patch_tokens, qkv, out_proj, up_proj, down_proj)
     return y[None]

time: 81.6 us -> 75.2 us (0.922)
  local copies, waits for them, and re-layouts: 8.06 us -> 1.57 us
    unnamed x17 -> x1, local copies, waits for them, and re-layouts: 8.06 us -> 1.57 us
where the time goes in v2:
time: 75.2 us; the launch traced here: 75.1 us
  Pallas kernels  73.5 us (98%)
  local copies, waits for them, and re-layouts  1.57 us (2%)
    pallas_call x1, Pallas kernels, shards(): pl.pallas_call(functools.partial(kernel, n_seq, chunks), name='encoder_la...  73.5 us
    unnamed x1, local copies, waits for them, and re-layouts  1.57 us

profile of v2, /device:TPU:1, one launch (start us, length us, event | category | flops | bytes accessed | tf_op | source)
XLA Modules:
  0.0 75.1 jit_solution(3076610121517657570)
XLA Ops:
  0.0 73.5 %encoder_layer.1 = bf16[64,1024]{1,0:T(8,128)(2,1)} custom-call(s32[1,16]{1,0:T(1,128)} %tile_hbm.1, s32[1,256]{1,0:T(1,128)} %keep_hbm.1, s32[1,256]{1,0:T(1,128)} %slot_hbm.1, f32[1,256]{1,0:T(1,128)} %constant.8.freq_hbm, bf16[1,256,1024]{2,1,0:T(8,128)(2,1)} %patch_hbm.1, bf16[3,1024,512]{2,1,0:T(8,128)(2,1)} %bitcast.4, bf16[1024,1024]{1,0:T(8,128)(2,1)} %out_hbm.1, ...), custom_call_target="tpu_custom_call" | custom-call | tf_op jit(solution)/shard_map/encoder_layer/pallas_call | solution.py:359
  73.5 1.6 %copy.11 = bf16[1,64,1024]{2,1,0:T(8,128)(2,1)} copy(bf16[1,64,1024]{2,1,0:T(8,128)(2,1)} %bitcast.5) | data formatting | bytes 262144

commit v3 on v2

--- a/solution.py
+++ b/solution.py
@@ -50,16 +50,20 @@
     f_right, f_left, f_far = lax.rem(f + 2, 8), lax.rem(f + 6, 8), lax.rem(f + 4, 8)
     mate = f + 1 - 2 * lax.rem(f, 2)
     m_right, m_left, m_far = lax.rem(mate + 2, 8), lax.rem(mate + 6, 8), lax.rem(mate + 4, 8)
-    s_next = lax.rem(s + 1, n_seq)
+    block_in = lax.rem(s + n_seq - c, n_seq)
     s_diag = lax.rem(s + n_seq + 2 * c - 1, n_seq)
 
     barrier = pltpu.get_barrier_semaphore()
 
+    def far_first(i):
+        return n_seq // 2 + (i + 1) // 2 * (2 * lax.rem(i, 2) - 1)
+
     def greet(i, carry):
-        pl.semaphore_signal(barrier, inc=1, device_id={"seq": lax.rem(s + i, n_seq)}, device_id_type=MESH)
+        peer = lax.rem(s + far_first(i), n_seq)
+        pl.semaphore_signal(barrier, inc=1, device_id={"seq": peer}, device_id_type=MESH)
         return carry
 
-    lax.fori_loop(1, n_seq, greet, 0)
+    lax.fori_loop(0, n_seq - 1, greet, 0)
     for peer in (f_right, f_left, mate):
         pl.semaphore_signal(barrier, inc=1, device_id={"fsdp": peer}, device_id_type=MESH)
     pl.semaphore_signal(barrier, inc=1, device_id={"canvas": other}, device_id_type=MESH)
@@ -127,14 +131,14 @@
     pl.semaphore_wait(barrier, n_seq + 4)
 
     def push(i, carry):
-        step = 32 + (i + 1) // 2 * (2 * lax.rem(i, 2) - 1)
-        to = lax.rem(s + step, n_seq)
+        to = lax.rem(s + far_first(i), n_seq)
+        block = lax.rem(to + n_seq - c, n_seq)
         pltpu.make_async_remote_copy(
             src_ref=lab_out, dst_ref=lab_in.at[s], send_sem=a2a_sem.at[0], recv_sem=a2a_sem.at[1],
             device_id={"seq": to}, device_id_type=MESH,
         ).start()
         pltpu.make_async_remote_copy(
-            src_ref=send.at[to], dst_ref=recv.at[s], send_sem=a2a_sem.at[2], recv_sem=a2a_sem.at[3],
+            src_ref=send.at[block], dst_ref=recv.at[s], send_sem=a2a_sem.at[2], recv_sem=a2a_sem.at[3],
             device_id={"seq": to}, device_id_type=MESH,
         ).start()
         return carry
@@ -142,34 +146,41 @@
     lax.fori_loop(0, n_seq - 1, push, 0)
     own_label = pltpu.make_async_copy(lab_out, lab_in.at[s], a2a_sem.at[4])
     own_label.start()
-    own_rows = pltpu.make_async_copy(send.at[s], recv.at[s], a2a_sem.at[5])
+    own_rows = pltpu.make_async_copy(send.at[block_in], recv.at[s], a2a_sem.at[5])
     own_rows.start()
 
-    def ship(src, buf, shard, to, index_s, index_r):
+    def piece(buf, shard, part):
+        first_row, count = ((0, 64), (64, 64), (0, 128))[part]
+        return buf.at[pl.ds(pl.multiple_of(shard * 128 + first_row, 64), count)]
+
+    shipped = []
+
+    def ship(buf, shard, part, to, index_r):
         copy = pltpu.make_async_remote_copy(
-            src_ref=src, dst_ref=buf.at[rows_of(shard)], send_sem=w_ssem.at[index_s], recv_sem=w_rsem.at[index_r],
+            src_ref=piece(buf, shard, part), dst_ref=piece(buf, shard, part),
+            send_sem=w_ssem.at[len(shipped)], recv_sem=w_rsem.at[index_r],
             device_id={"fsdp": to}, device_id_type=MESH,
         )
         copy.start()
-        return copy
-
-    def landed(buf, shard, index_r):
-        view = buf.at[rows_of(shard)]
+        shipped.append(copy)
+
+    def landed(buf, shard, part, index_r):
+        view = piece(buf, shard, part)
         pltpu.make_async_copy(view, view, w_rsem.at[index_r]).wait()
 
-    shipped = [
-        ship(up_hbm, up_v, f, f_right, 0, 0),
-        ship(down_hbm, down_v, f, f_left, 1, 3),
-        ship(down_hbm, down_v, f, f_right, 2, 1),
-        ship(up_hbm, up_v, f, f_left, 3, 2),
-        ship(up_hbm, up_v, f, mate, 4, 6),
-        ship(down_hbm, down_v, f, mate, 5, 7),
-    ]
+    up_load.wait()
+    ship(up_v, f, 2, f_right, 0)
+    ship(up_v, f, 2, f_left, 1)
+    ship(up_v, f, 2, mate, 10)
+    down_load.wait()
+    ship(down_v, f, 0, f_right, 2)
+    ship(down_v, f, 1, f_left, 5)
+    ship(down_v, f, 2, mate, 11)
 
     own_label.wait()
     pltpu.make_async_copy(lab_in.at[pl.ds(0, n_seq - 1)], lab_in.at[pl.ds(0, n_seq - 1)], a2a_sem.at[1]).wait()
     lane_of = lax.broadcasted_iota(jnp.int32, (8, 128), 1)
-    mine = jnp.where(lane_of == s, 1.0, 0.0).astype(BF16)
+    mine = jnp.where(lane_of == block_in, 1.0, 0.0).astype(BF16)
     came = matmul_nt(mine, lab_in[...].reshape(n_seq, 128).astype(BF16))
     spread_r = lax.broadcasted_iota(jnp.int32, (n_seq, 512), 0)
     spread_c = lax.broadcasted_iota(jnp.int32, (n_seq, 512), 1)
@@ -183,88 +194,78 @@
     for h in range(2):
         row_h = jnp.where(half_of == h, row_of, -1)[0:1, :]
         places.append(jnp.where(r_i == row_h, 1.0, 0.0).astype(BF16))
+    landed(up_v, f_left, 2, 0)
+    ship(up_v, f_left, 0, f_right, 6)
+    landed(up_v, f_right, 2, 1)
+    ship(up_v, f_right, 1, f_left, 7)
+    ship(down_v, f, 1, f_right, 3)
+    ship(down_v, f, 0, f_left, 4)
+
     own_rows.wait()
     pltpu.make_async_copy(recv.at[pl.ds(0, n_seq - 1)], recv.at[pl.ds(0, n_seq - 1)], a2a_sem.at[3]).wait()
     came_rows = recv[...].reshape(512, QUART)
-    for h in range(2):
-        vis[0, c, :, h * QUART:(h + 1) * QUART] = matmul(places[h], came_rows).astype(BF16)
-
     size = 128 // chunks
 
     def view_of(block, half, k):
         return vis.at[block, half, pl.ds(k * size, size), :]
 
-    def pass_on(half, src_block, dst_block, k, to, index_s, index_r):
-        copy = pltpu.make_async_remote_copy(
-            src_ref=view_of(src_block, half, k), dst_ref=view_of(dst_block, half, k),
-            send_sem=vis_ssem.at[index_s * chunks + k], recv_sem=vis_rsem.at[index_r * chunks + k],
+    def pass_on(block, half, to_block, k, to, leg):
+        pltpu.make_async_remote_copy(
+            src_ref=view_of(block, half, k), dst_ref=view_of(to_block, half, k),
+            send_sem=vis_ssem.at[leg * chunks + k], recv_sem=vis_rsem.at[leg * chunks + k],
             device_id=to, device_id_type=MESH,
-        )
-        copy.start()
-        return copy
-
-    def arrived(block, half, k, index_r):
+        ).start()
+
+    def arrived(block, half, k, leg):
         view = view_of(block, half, k)
-        pltpu.make_async_copy(view, view, vis_rsem.at[index_r * chunks + k]).wait()
-
-    def sent(half, k, index_s):
-        view = view_of(0, half, k)
-        pltpu.make_async_copy(view, view, vis_ssem.at[index_s * chunks + k]).wait()
+        pltpu.make_async_copy(view, view, vis_rsem.at[leg * chunks + k]).wait()
+
+    def sent(k, leg):
+        view = view_of(0, 0, k)
+        pltpu.make_async_copy(view, view, vis_ssem.at[leg * chunks + k]).wait()
 
     pair = {"canvas": other}
-    onward = {"seq": s_next, "canvas": 0}
+    diagonal = {"seq": s_diag, "canvas": other}
     for k in range(chunks):
-        pass_on(c, 0, 0, k, pair, 0, 0)
-
-    @pl.when(c == 1)
-    def _():
-        for k in range(chunks):
-            pass_on(1, 0, 1, k, onward, 1, 1)
-        for k in range(chunks):
-            arrived(0, 0, k, 0)
-            pass_on(0, 0, 1, k, onward, 2, 2)
-
-    @pl.when(c == 0)
-    def _():
-        for k in range(chunks):
-            arrived(1, 1, k, 1)
-            pass_on(1, 1, 1, k, pair, 1, 1)
-        for k in range(chunks):
-            arrived(0, 1, k, 0)
-
-    landed(up_v, f_left, 0)
-    shipped.append(ship(up_v.at[rows_of(f_left)], up_v, f_left, f_right, 6, 4))
-    landed(down_v, f_right, 3)
-    shipped.append(ship(down_v.at[rows_of(f_right)], down_v, f_right, f_left, 7, 5))
-    shipped.append(ship(up_v.at[rows_of(f_left)], up_v, f_left, mate, 8, 8))
-    shipped.append(ship(down_v.at[rows_of(f_right)], down_v, f_right, mate, 9, 11))
+        for h in range(2):
+            place = places[h][k * size:(k + 1) * size, :]
+            vis[c, c, k * size:(k + 1) * size, h * QUART:(h + 1) * QUART] = matmul(place, came_rows).astype(BF16)
+        pass_on(c, c, c, k, pair, 0)
+    ship(up_v, f_left, 2, mate, 12)
+    ship(up_v, f_right, 2, mate, 13)
+    for k in range(chunks):
+        arrived(other, other, k, 0)
+        pass_on(other, other, c, k, diagonal, 1)
+    for k in range(chunks):
+        arrived(other, c, k, 1)
+        pass_on(other, c, other, k, pair, 2)
 
     qkv_load.wait()
-    visible = jnp.concatenate([vis[0, 0], vis[0, 1]], axis=1).astype(F32)
-    normed[...] = normalised(visible).astype(BF16)
-    q_s[...] = matmul(normed[...], qkv_v[0]).astype(BF16)
-    k_s[0:128, :] = matmul(normed[...], qkv_v[1]).astype(BF16)
-    v_s[0:128, :] = matmul(normed[...], qkv_v[2]).astype(BF16)
-
-    @pl.when(c == 0)
-    def _():
-        for k in range(chunks):
-            arrived(1, 0, k, 2)
-            pass_on(0, 1, 1, k, pair, 2, 2)
-
-    @pl.when(c == 1)
-    def _():
-        for k in range(chunks):
-            arrived(1, 1, k, 1)
-        for k in range(chunks):
-            arrived(1, 0, k, 2)
-
-    before = jnp.concatenate([vis[1, 0], vis[1, 1]], axis=1).astype(F32)
-    normed[...] = normalised(before).astype(BF16)
-    k_s[128:256, :] = matmul(normed[...], qkv_v[1]).astype(BF16)
-    v_s[128:256, :] = matmul(normed[...], qkv_v[2]).astype(BF16)
+
+    def project(block):
+        rows = pl.ds(pl.multiple_of(block * 128, 128), 128)
+        normed[...] = normalised(jnp.concatenate([vis[block, 0], vis[block, 1]], axis=1).astype(F32)).astype(BF16)
+        k_s[rows, :] = matmul(normed[...], qkv_v[1]).astype(BF16)
+        v_s[rows, :] = matmul(normed[...], qkv_v[2]).astype(BF16)
+
+        @pl.when(block == 0)
+        def _():
+            q_s[...] = matmul(normed[...], qkv_v[0]).astype(BF16)
+
+    project(other)
+    landed(up_v, f_far, 0, 6)
+    landed(up_v, f_far, 1, 7)
+    ship(up_v, f_far, 2, mate, 16)
+    landed(down_v, f_left, 0, 2)
+    ship(down_v, f_left, 0, f_right, 8)
+    landed(down_v, f_right, 1, 5)
+    ship(down_v, f_right, 1, f_left, 9)
+    for k in range(chunks):
+        arrived(c, other, k, 2)
+    project(c)
 
     low = lax.broadcasted_iota(jnp.int32, (128, 128), 1) < 64
+    att_copies = []
     for p in range(4):
         lanes = pl.ds(p * 128, 128)
         q_pair, k_pair, v_pair = q_s[:, lanes], k_s[:, lanes], v_s[:, lanes]
@@ -275,37 +276,37 @@
             expo = jnp.exp(scores - jnp.max(scores, axis=-1, keepdims=True))
             total = jnp.sum(expo, axis=-1, keepdims=True)
             mixed.append(matmul(expo.astype(BF16), v_pair) / total)
-        att[c, :, lanes] = jnp.where(low, mixed[0], mixed[1]).astype(BF16)
-
-    att_copy = pltpu.make_async_remote_copy(
-        src_ref=att.at[c], dst_ref=att.at[c], send_sem=att_sem.at[0], recv_sem=att_sem.at[1],
-        device_id=pair, device_id_type=MESH,
-    )
-    att_copy.start()
-
-    landed(down_v, f_left, 1)
-    shipped.append(ship(down_v.at[rows_of(f_left)], down_v, f_left, mate, 10, 9))
-    landed(up_v, f_right, 2)
-    shipped.append(ship(up_v.at[rows_of(f_right)], up_v, f_right, mate, 11, 10))
+        att[c, p] = jnp.where(low, mixed[0], mixed[1]).astype(BF16)
+        copy = pltpu.make_async_remote_copy(
+            src_ref=att.at[c, p], dst_ref=att.at[c, p], send_sem=att_sem.at[p], recv_sem=att_sem.at[4 + p],
+            device_id=pair, device_id_type=MESH,
+        )
+        copy.start()
+        att_copies.append(copy)
+
+    landed(down_v, f_left, 1, 3)
+    ship(down_v, f_left, 2, mate, 14)
+    landed(down_v, f_right, 0, 4)
+    ship(down_v, f_right, 2, mate, 15)
 
     out_load.wait()
-    att_copy.wait_recv()
-    mixed_in = jnp.concatenate([att[0], att[1]], axis=1)
+
+    def mix(half):
+        rows = pl.ds(pl.multiple_of(half * HALF, HALF), HALF)
+        heads = jnp.concatenate([att[half, p] for p in range(4)], axis=1)
+        return matmul(heads, out_v[rows, :])
+
     visible = jnp.concatenate([vis[0, 0], vis[0, 1]], axis=1).astype(F32)
-    resid[...] = visible + matmul(mixed_in, out_v[...])
+    resid[...] = visible + mix(c)
+    for copy in att_copies:
+        copy.wait_recv()
+    resid[...] += mix(other)
     normed2[...] = normalised(resid[...]).astype(BF16)
 
-    landed(up_v, f_far, 4)
-    shipped.append(ship(up_v.at[rows_of(f_far)], up_v, f_far, mate, 12, 12))
-    landed(down_v, f_far, 5)
-    shipped.append(ship(down_v.at[rows_of(f_far)], down_v, f_far, mate, 13, 13))
-
-    up_load.wait()
-    down_load.wait()
-    landed(up_v, mate, 6)
-    landed(up_v, m_left, 8)
-    landed(up_v, m_right, 10)
-    landed(up_v, m_far, 12)
+    landed(up_v, mate, 2, 10)
+    landed(up_v, m_left, 2, 12)
+    landed(up_v, m_right, 2, 13)
+    landed(up_v, m_far, 2, 16)
 
     def widen(n, carry):
         cols = pl.ds(pl.multiple_of(n * 256, 256), 256)
@@ -314,17 +315,18 @@
 
     lax.fori_loop(0, 8, widen, 0)
 
-    landed(down_v, mate, 7)
-    landed(down_v, m_left, 9)
-    landed(down_v, m_right, 11)
-    landed(down_v, m_far, 13)
+    landed(down_v, f_far, 0, 8)
+    landed(down_v, f_far, 1, 9)
+    ship(down_v, f_far, 2, mate, 17)
 
     here = pl.ds(pl.multiple_of(c * 64, 64), 64)
     there = pl.ds(pl.multiple_of(other * 64, 64), 64)
+    chip = f // 2
     y_copies = []
-    for n in range(4):
-        cols = pl.ds(n * 256, 256)
-        part[:, cols] = matmul_nt(hidden[...], down_v[n * 256:(n + 1) * 256, :])
+    for n, (step, shard, index_r) in enumerate(((0, mate, 11), (3, m_left, 14), (1, m_right, 15), (2, m_far, 17))):
+        landed(down_v, shard, 2, index_r)
+        cols = pl.ds(pl.multiple_of(lax.rem(chip + step, 4) * 256, 256), 256)
+        part[:, cols] = matmul_nt(hidden[...], down_v[cols, :])
         y_out[n] = part[there, cols].astype(BF16)
         copy = pltpu.make_async_remote_copy(
             src_ref=y_out.at[n], dst_ref=y_in.at[n], send_sem=y_ssem.at[n], recv_sem=y_rsem.at[n],
@@ -332,21 +334,20 @@
         )
         copy.start()
         y_copies.append(copy)
-    for n in range(4):
-        cols = pl.ds(n * 256, 256)
+    for n, step in enumerate((0, 3, 1, 2)):
+        cols = pl.ds(pl.multiple_of(lax.rem(chip + step, 4) * 256, 256), 256)
         y_copies[n].wait_recv()
         y_ref[:, cols] = (resid[here, cols] + part[here, cols] + y_in[n].astype(F32)).astype(BF16)
 
     first63 = pl.ds(0, n_seq - 1)
     pltpu.make_async_copy(lab_in.at[first63], lab_in.at[first63], a2a_sem.at[0]).wait()
     pltpu.make_async_copy(send.at[first63], send.at[first63], a2a_sem.at[2]).wait()
-    for index_s in range(3):
+    for leg in range(3):
         for k in range(chunks):
-            sent(0, k, index_s)
+            sent(k, leg)
     for copy in shipped:
         copy.wait_send()
-    att_copy.wait_send()
-    for copy in y_copies:
+    for copy in att_copies + y_copies:
         copy.wait_send()
 
 
@@ -359,7 +360,7 @@
     y = pl.pallas_call(
         functools.partial(kernel, n_seq, chunks),
         name="encoder_layer",
-        out_shape=jax.ShapeDtypeStruct((64, D), BF16),
+        out_shape=pltpu.VMEM((64, D), BF16),
         in_specs=[hbm] * 9,
         out_specs=vmem,
         scratch_shapes=[
@@ -382,7 +383,7 @@
             pltpu.VMEM((128, HALF), BF16),
             pltpu.VMEM((256, HALF), BF16),
             pltpu.VMEM((256, HALF), BF16),
-            pltpu.VMEM((2, 128, HALF), BF16),
+            pltpu.VMEM((2, 4, 128, 128), BF16),
             pltpu.VMEM((128, D), F32),
             pltpu.VMEM((128, D), BF16),
             pltpu.VMEM((128, 2048), BF16),
@@ -393,16 +394,19 @@
             pltpu.SemaphoreType.DMA((6,)),
             pltpu.SemaphoreType.DMA((3 * chunks,)),
             pltpu.SemaphoreType.DMA((3 * chunks,)),
-            pltpu.SemaphoreType.DMA((14,)),
-            pltpu.SemaphoreType.DMA((14,)),
-            pltpu.SemaphoreType.DMA((2,)),
+            pltpu.SemaphoreType.DMA((18,)),
+            pltpu.SemaphoreType.DMA((18,)),
+            pltpu.SemaphoreType.DMA((8,)),
             pltpu.SemaphoreType.DMA((4,)),
             pltpu.SemaphoreType.DMA((4,)),
         ],
         compiler_params=pltpu.CompilerParams(
-            collective_id=0, has_side_effects=True, vmem_limit_bytes=67043328
+            collective_id=0, has_side_effects=True, vmem_limit_bytes=58 * 1024 * 1024
         ),
-    )(tile_map, keep_mask, slot_index, freq, patch_tokens, qkv, out_proj, up_proj, down_proj)
+    )(*[
+        pltpu.with_memory_space_constraint(operand, pltpu.HBM)
+        for operand in (tile_map, keep_mask, slot_index, freq, patch_tokens, qkv, out_proj, up_proj, down_proj)
+    ])
     return y[None]
 
 
@@ -418,7 +422,7 @@
         P("fsdp", "canvas"),
     )
     return jax.shard_map(
-        functools.partial(shards, 2),
+        functools.partial(shards, 4),
         mesh=mesh,
         in_specs=placed,
         out_specs=P("fsdp", ("seq", "canvas"), None),

time: 75.2 us -> 70.1 us (0.932)
  Pallas kernels: 73.5 us -> 69.3 us
  local copies, waits for them, and re-layouts: 1.57 us -> 0.66 us
    pallas_call x1, Pallas kernels: 73.5 us -> 69.3 us  [shards(): pl.pallas_call(functools.partial(kernel, n_seq, chunks), name='encoder_la...]
    unnamed x1, local copies, waits for them, and re-layouts: 1.57 us -> 0.66 us
where the time goes in v3:
time: 70.1 us; the launch traced here: 70 us
  Pallas kernels  69.3 us (99%)
    pallas_call x1, Pallas kernels, shards(): pl.pallas_call(functools.partial(kernel, n_seq, chunks), name='encoder_la...  69.3 us

profile of v3, /device:TPU:1, one launch (start us, length us, event | category | flops | bytes accessed | tf_op | source)
XLA Modules:
  0.0 70.0 jit_solution(703077236816223528)
XLA Ops:
  0.0 69.3 %encoder_layer.1 = bf16[64,1024]{1,0:T(8,128)(2,1)S(1)} custom-call(s32[1,16]{1,0:T(1,128)} %tile_hbm.1, s32[1,256]{1,0:T(1,128)} %keep_hbm.1, s32[1,256]{1,0:T(1,128)} %slot_hbm.1, f32[1,256]{1,0:T(1,128)} %constant.8.freq_hbm, bf16[1,256,1024]{2,1,0:T(8,128)(2,1)} %patch_hbm.1, bf16[3,1024,512]{2,1,0:T(8,128)(2,1)} %bitcast.5, bf16[1024,1024]{1,0:T(8,128)(2,1)} %out_hbm.1, ...), custom_call_target="tpu_custom_call" | custom-call | tf_op jit(solution)/shard_map/encoder_layer/pallas_call | solution.py:360
  69.3 0.7 copy.11

commit v4 on v3

--- a/solution.py
+++ b/solution.py
@@ -41,7 +41,7 @@
     y_ref,
     tile_ref, keep_ref, slot_ref, freq_ref, patch_v, qkv_v, out_v, up_v, down_v,
     emb, send, recv, lab_out, lab_in, vis, normed, q_s, k_s, v_s, att, resid, normed2, hidden, part, y_out, y_in,
-    load_sem, a2a_sem, vis_ssem, vis_rsem, w_ssem, w_rsem, att_sem, y_ssem, y_rsem,
+    met_sem, load_sem, a2a_sem, vis_ssem, vis_rsem, w_ssem, w_rsem, att_sem, y_ssem, y_rsem,
 ):
     s = lax.axis_index("seq")
     f = lax.axis_index("fsdp")
@@ -54,16 +54,26 @@
     s_diag = lax.rem(s + n_seq + 2 * c - 1, n_seq)
 
     barrier = pltpu.get_barrier_semaphore()
-
-    def far_first(i):
-        return n_seq // 2 + (i + 1) // 2 * (2 * lax.rem(i, 2) - 1)
-
-    def greet(i, carry):
-        peer = lax.rem(s + far_first(i), n_seq)
-        pl.semaphore_signal(barrier, inc=1, device_id={"seq": peer}, device_id_type=MESH)
+    n_z = n_seq // 4
+    z, y_hi = s // 4, lax.rem(s, 4)
+    n_near, n_far = n_seq // 2 + 3, n_seq // 2 - 4
+
+    def peer_at(dz, dy):
+        return lax.rem(z + dz + n_z, n_z) * 4 + lax.rem(y_hi + dy, 4)
+
+    def near_peer(j):
+        i = j // 4
+        return peer_at((n_z // 4 - i // 2) * (1 - 2 * lax.rem(i, 2)), j + 1)
+
+    def far_peer(j):
+        i = j // 4
+        return peer_at((n_z // 2 - (i + 1) // 2) * (1 - 2 * lax.rem(i, 2)), j)
+
+    def greet(j, carry):
+        pl.semaphore_signal(barrier, inc=1, device_id={"seq": near_peer(j)}, device_id_type=MESH)
         return carry
 
-    lax.fori_loop(0, n_seq - 1, greet, 0)
+    lax.fori_loop(0, n_near, greet, 0)
     for peer in (f_right, f_left, mate):
         pl.semaphore_signal(barrier, inc=1, device_id={"fsdp": peer}, device_id_type=MESH)
     pl.semaphore_signal(barrier, inc=1, device_id={"canvas": other}, device_id_type=MESH)
@@ -108,17 +118,26 @@
     freq = freq_ref[...]
     within = lax.broadcasted_iota(jnp.int32, (16, QUART), 0)
     cell = jnp.where(c == 0, within // 4, lax.rem(within, 4))
-
-    def embed(t, carry):
+    two_tiles = lax.broadcasted_iota(jnp.int32, (8, QUART), 0)
+
+    def corner(t):
         tile = tile_ref[0, t]
-        base = jnp.where(c == 0, tile // 32, lax.rem(tile, 32)) * 4
-        angle = (base + cell).astype(F32) * freq
-        rows = pl.ds(pl.multiple_of(t * 16, 16), 16)
-        emb[0, rows, :] = (patch_v[rows, 0:QUART].astype(F32) + jnp.sin(angle)).astype(BF16)
-        emb[1, rows, :] = (patch_v[rows, QUART:HALF].astype(F32) + jnp.cos(angle)).astype(BF16)
+        return jnp.where(c == 0, tile // 32, lax.rem(tile, 32)) * 4
+
+    def embed(pair_at, carry):
+        base = jnp.where(two_tiles < 4, corner(pair_at * 2), corner(pair_at * 2 + 1) - 4)
+        angle = (base + two_tiles).astype(F32) * freq
+        for quarter, table in enumerate((jnp.sin(angle), jnp.cos(angle))):
+            for e in range(2):
+                rows = pl.ds(pl.multiple_of(pair_at * 32 + e * 16, 16), 16)
+                added = jnp.broadcast_to(table[e * 4:e * 4 + 1, :], (16, QUART))
+                for k in range(1, 4):
+                    added = jnp.where(cell == k, table[e * 4 + k:e * 4 + k + 1, :], added)
+                tokens = patch_v[rows, quarter * QUART:(quarter + 1) * QUART].astype(F32)
+                emb[quarter, rows, :] = (tokens + added).astype(BF16)
         return carry
 
-    lax.fori_loop(0, 16, embed, 0)
+    lax.fori_loop(0, 8, embed, 0)
 
     key = jnp.where(kept, target * 4 + lane4, -1000)
     row_i = lax.broadcasted_iota(jnp.int32, (512, QUART), 0)
@@ -128,10 +147,11 @@
     packed = matmul(pick0, emb[0]) + matmul(pick1, emb[1])
     send[...] = packed.astype(BF16).reshape(n_seq, 8, QUART)
 
-    pl.semaphore_wait(barrier, n_seq + 4)
-
-    def push(i, carry):
-        to = lax.rem(s + far_first(i), n_seq)
+    pl.semaphore_wait(barrier, n_near + 5)
+    for dz in (n_z // 4, -(n_z // 4)):
+        pl.semaphore_signal(met_sem, inc=1, device_id={"seq": peer_at(dz, 0)}, device_id_type=MESH)
+
+    def push(to):
         block = lax.rem(to + n_seq - c, n_seq)
         pltpu.make_async_remote_copy(
             src_ref=lab_out, dst_ref=lab_in.at[s], send_sem=a2a_sem.at[0], recv_sem=a2a_sem.at[1],
@@ -141,9 +161,16 @@
             src_ref=send.at[block], dst_ref=recv.at[s], send_sem=a2a_sem.at[2], recv_sem=a2a_sem.at[3],
             device_id={"seq": to}, device_id_type=MESH,
         ).start()
+
+    def push_near(j, carry):
+        push(near_peer(j))
         return carry
 
-    lax.fori_loop(0, n_seq - 1, push, 0)
+    def push_far(j, carry):
+        push(far_peer(j))
+        return carry
+
+    lax.fori_loop(0, n_near, push_near, 0)
     own_label = pltpu.make_async_copy(lab_out, lab_in.at[s], a2a_sem.at[4])
     own_label.start()
     own_rows = pltpu.make_async_copy(send.at[block_in], recv.at[s], a2a_sem.at[5])
@@ -176,6 +203,9 @@
     ship(down_v, f, 0, f_right, 2)
     ship(down_v, f, 1, f_left, 5)
     ship(down_v, f, 2, mate, 11)
+
+    pl.semaphore_wait(met_sem, 2)
+    lax.fori_loop(0, n_far, push_far, 0)
 
     own_label.wait()
     pltpu.make_async_copy(lab_in.at[pl.ds(0, n_seq - 1)], lab_in.at[pl.ds(0, n_seq - 1)], a2a_sem.at[1]).wait()
@@ -390,6 +420,7 @@
             pltpu.VMEM((128, D), F32),
             pltpu.VMEM((4, 64, 256), BF16),
             pltpu.VMEM((4, 64, 256), BF16),
+            pltpu.SemaphoreType.REGULAR,
             pltpu.SemaphoreType.DMA((9,)),
             pltpu.SemaphoreType.DMA((6,)),
             pltpu.SemaphoreType.DMA((3 * chunks,)),

time: 70.1 us -> 69.6 us (level)
  Pallas kernels: 69.3 us -> 68.1 us
    pallas_call x1, Pallas kernels: 69.3 us -> 68.1 us  [shards(): pl.pallas_call(functools.partial(kernel, n_seq, chunks), name='encoder_la...]
where the time goes in v4:
time: 69.6 us; the launch traced here: 68.8 us
  Pallas kernels  68.1 us (98%)
    pallas_call x1, Pallas kernels, shards(): pl.pallas_call(functools.partial(kernel, n_seq, chunks), name='encoder_la...  68.1 us

profile of v4, /device:TPU:1, one launch (start us, length us, event | category | flops | bytes accessed | tf_op | source)
XLA Modules:
  0.0 68.8 jit_solution(3956328514685628110)
XLA Ops:
  0.0 68.1 %encoder_layer.1 = bf16[64,1024]{1,0:T(8,128)(2,1)S(1)} custom-call(s32[1,16]{1,0:T(1,128)} %tile_hbm.1, s32[1,256]{1,0:T(1,128)} %keep_hbm.1, s32[1,256]{1,0:T(1,128)} %slot_hbm.1, f32[1,256]{1,0:T(1,128)} %constant.8.freq_hbm, bf16[1,256,1024]{2,1,0:T(8,128)(2,1)} %patch_hbm.1, bf16[3,1024,512]{2,1,0:T(8,128)(2,1)} %bitcast.5, bf16[1024,1024]{1,0:T(8,128)(2,1)} %out_hbm.1, ...), custom_call_target="tpu_custom_call" | custom-call | tf_op jit(solution)/shard_map/encoder_layer/pallas_call | solution.py:390
  68.1 0.7 copy.11

commit v5 on v4

--- a/solution.py
+++ b/solution.py
@@ -40,8 +40,8 @@
     tile_hbm, keep_hbm, slot_hbm, freq_hbm, patch_hbm, qkv_hbm, out_hbm, up_hbm, down_hbm,
     y_ref,
     tile_ref, keep_ref, slot_ref, freq_ref, patch_v, qkv_v, out_v, up_v, down_v,
-    emb, send, recv, lab_out, lab_in, vis, normed, q_s, k_s, v_s, att, resid, normed2, hidden, part, y_out, y_in,
-    met_sem, load_sem, a2a_sem, vis_ssem, vis_rsem, w_ssem, w_rsem, att_sem, y_ssem, y_rsem,
+    emb, send, mid, recv, lab_out, lab_mid, lab_in, vis, normed, q_s, k_s, v_s, att, resid, normed2, hidden, part, y_out, y_in,
+    met_sem, load_sem, a2a_sem, y_sem, vis_ssem, vis_rsem, w_ssem, w_rsem, att_sem, y_ssem, y_rsem,
 ):
     s = lax.axis_index("seq")
     f = lax.axis_index("fsdp")
@@ -56,24 +56,22 @@
     barrier = pltpu.get_barrier_semaphore()
     n_z = n_seq // 4
     z, y_hi = s // 4, lax.rem(s, 4)
-    n_near, n_far = n_seq // 2 + 3, n_seq // 2 - 4
 
     def peer_at(dz, dy):
         return lax.rem(z + dz + n_z, n_z) * 4 + lax.rem(y_hi + dy, 4)
 
-    def near_peer(j):
-        i = j // 4
-        return peer_at((n_z // 4 - i // 2) * (1 - 2 * lax.rem(i, 2)), j + 1)
-
-    def far_peer(j):
-        i = j // 4
-        return peer_at((n_z // 2 - (i + 1) // 2) * (1 - 2 * lax.rem(i, 2)), j)
+    def far_first(j, reach):
+        return (reach - (j + 1) // 2) * (1 - 2 * lax.rem(j, 2))
+
+    for dy in (2, 1, 3):
+        pl.semaphore_signal(barrier, inc=1, device_id={"seq": peer_at(0, dy)}, device_id_type=MESH)
 
     def greet(j, carry):
-        pl.semaphore_signal(barrier, inc=1, device_id={"seq": near_peer(j)}, device_id_type=MESH)
+        dz = (n_z // 4 - j // 2) * (1 - 2 * lax.rem(j, 2))
+        pl.semaphore_signal(barrier, inc=1, device_id={"seq": peer_at(dz, 0)}, device_id_type=MESH)
         return carry
 
-    lax.fori_loop(0, n_near, greet, 0)
+    lax.fori_loop(0, n_z // 2, greet, 0)
     for peer in (f_right, f_left, mate):
         pl.semaphore_signal(barrier, inc=1, device_id={"fsdp": peer}, device_id_type=MESH)
     pl.semaphore_signal(barrier, inc=1, device_id={"canvas": other}, device_id_type=MESH)
@@ -141,40 +139,37 @@
 
     key = jnp.where(kept, target * 4 + lane4, -1000)
     row_i = lax.broadcasted_iota(jnp.int32, (512, QUART), 0)
-    row_key = row_i // 8 * 4 + lax.rem(row_i, 4) + lax.rem(row_i // 4, 2) * 256
+    slot_i = row_i // 8
+    block_i = lax.rem(lax.rem(slot_i, n_z) * 4 + slot_i // n_z + n_seq - c, n_seq)
+    row_key = block_i * 4 + lax.rem(row_i, 4) + lax.rem(row_i // 4, 2) * 256
     pick0 = jnp.where(row_key == key, 1.0, 0.0).astype(BF16)
     pick1 = jnp.where(row_key == key + 256, 1.0, 0.0).astype(BF16)
     packed = matmul(pick0, emb[0]) + matmul(pick1, emb[1])
-    send[...] = packed.astype(BF16).reshape(n_seq, 8, QUART)
-
-    pl.semaphore_wait(barrier, n_near + 5)
+    send[...] = packed.astype(BF16).reshape(4, n_z, 8, QUART)
+
+    pl.semaphore_wait(barrier, n_z // 2 + 8)
     for dz in (n_z // 4, -(n_z // 4)):
         pl.semaphore_signal(met_sem, inc=1, device_id={"seq": peer_at(dz, 0)}, device_id_type=MESH)
 
-    def push(to):
-        block = lax.rem(to + n_seq - c, n_seq)
+    own_label = pltpu.make_async_copy(lab_out, lab_mid.at[y_hi], a2a_sem.at[4])
+    own_label.start()
+    own_rows = pltpu.make_async_copy(send.at[y_hi], mid.at[y_hi], a2a_sem.at[5])
+    own_rows.start()
+    for dy in (2, 1, 3):
         pltpu.make_async_remote_copy(
-            src_ref=lab_out, dst_ref=lab_in.at[s], send_sem=a2a_sem.at[0], recv_sem=a2a_sem.at[1],
-            device_id={"seq": to}, device_id_type=MESH,
+            src_ref=lab_out, dst_ref=lab_mid.at[y_hi], send_sem=a2a_sem.at[0], recv_sem=a2a_sem.at[1],
+            device_id={"seq": peer_at(0, dy)}, device_id_type=MESH,
         ).start()
-        pltpu.make_async_remote_copy(
-            src_ref=send.at[block], dst_ref=recv.at[s], send_sem=a2a_sem.at[2], recv_sem=a2a_sem.at[3],
-            device_id={"seq": to}, device_id_type=MESH,
-        ).start()
-
-    def push_near(j, carry):
-        push(near_peer(j))
-        return carry
-
-    def push_far(j, carry):
-        push(far_peer(j))
-        return carry
-
-    lax.fori_loop(0, n_near, push_near, 0)
-    own_label = pltpu.make_async_copy(lab_out, lab_in.at[s], a2a_sem.at[4])
-    own_label.start()
-    own_rows = pltpu.make_async_copy(send.at[block_in], recv.at[s], a2a_sem.at[5])
-    own_rows.start()
+    n_part = n_z // 4
+    parts = [lax.rem(z // n_part + off, 4) for off in (2, 3, 1, 0)]
+    for q in parts:
+        column = pl.ds(q * n_part, n_part)
+        for dy in (2, 1, 3):
+            pltpu.make_async_remote_copy(
+                src_ref=send.at[lax.rem(y_hi + dy, 4), column], dst_ref=mid.at[y_hi, column],
+                send_sem=a2a_sem.at[2], recv_sem=y_sem.at[q],
+                device_id={"seq": peer_at(0, dy)}, device_id_type=MESH,
+            ).start()
 
     def piece(buf, shard, part):
         first_row, count = ((0, 64), (64, 64), (0, 128))[part]
@@ -205,10 +200,40 @@
     ship(down_v, f, 2, mate, 11)
 
     pl.semaphore_wait(met_sem, 2)
-    lax.fori_loop(0, n_far, push_far, 0)
-
     own_label.wait()
-    pltpu.make_async_copy(lab_in.at[pl.ds(0, n_seq - 1)], lab_in.at[pl.ds(0, n_seq - 1)], a2a_sem.at[1]).wait()
+    three = pl.ds(0, 3)
+    pltpu.make_async_copy(lab_mid.at[three], lab_mid.at[three], a2a_sem.at[1]).wait()
+    own_labels = pltpu.make_async_copy(lab_mid, lab_in.at[z], a2a_sem.at[8])
+    own_labels.start()
+
+    def push_labels(j, carry):
+        pltpu.make_async_remote_copy(
+            src_ref=lab_mid, dst_ref=lab_in.at[z], send_sem=a2a_sem.at[6], recv_sem=a2a_sem.at[7],
+            device_id={"seq": peer_at(far_first(j, n_z // 2), 0)}, device_id_type=MESH,
+        ).start()
+        return carry
+
+    lax.fori_loop(0, n_z - 1, push_labels, 0)
+    own_rows.wait()
+    for q in parts:
+        came = mid.at[three, pl.ds(q * n_part, n_part)]
+        pltpu.make_async_copy(came, came, y_sem.at[q]).wait()
+        for j in range(n_part):
+            to = q * n_part + j
+
+            @pl.when(to != z)
+            def _():
+                pltpu.make_async_remote_copy(
+                    src_ref=mid.at[:, to], dst_ref=recv.at[z], send_sem=a2a_sem.at[9], recv_sem=a2a_sem.at[3],
+                    device_id={"seq": to * 4 + y_hi}, device_id_type=MESH,
+                ).start()
+
+    own_column = pltpu.make_async_copy(mid.at[:, z], recv.at[z], a2a_sem.at[10])
+    own_column.start()
+
+    others = pl.ds(0, n_z - 1)
+    own_labels.wait()
+    pltpu.make_async_copy(lab_in.at[others], lab_in.at[others], a2a_sem.at[7]).wait()
     lane_of = lax.broadcasted_iota(jnp.int32, (8, 128), 1)
     mine = jnp.where(lane_of == block_in, 1.0, 0.0).astype(BF16)
     came = matmul_nt(mine, lab_in[...].reshape(n_seq, 128).astype(BF16))
@@ -231,8 +256,8 @@
     ship(down_v, f, 1, f_right, 3)
     ship(down_v, f, 0, f_left, 4)
 
-    own_rows.wait()
-    pltpu.make_async_copy(recv.at[pl.ds(0, n_seq - 1)], recv.at[pl.ds(0, n_seq - 1)], a2a_sem.at[3]).wait()
+    own_column.wait()
+    pltpu.make_async_copy(recv.at[others], recv.at[others], a2a_sem.at[3]).wait()
     came_rows = recv[...].reshape(512, QUART)
     size = 128 // chunks
 
@@ -369,9 +394,10 @@
         y_copies[n].wait_recv()
         y_ref[:, cols] = (resid[here, cols] + part[here, cols] + y_in[n].astype(F32)).astype(BF16)
 
-    first63 = pl.ds(0, n_seq - 1)
-    pltpu.make_async_copy(lab_in.at[first63], lab_in.at[first63], a2a_sem.at[0]).wait()
-    pltpu.make_async_copy(send.at[first63], send.at[first63], a2a_sem.at[2]).wait()
+    pltpu.make_async_copy(lab_mid.at[three], lab_mid.at[three], a2a_sem.at[0]).wait()
+    pltpu.make_async_copy(send.at[three], send.at[three], a2a_sem.at[2]).wait()
+    pltpu.make_async_copy(lab_in.at[others], lab_in.at[others], a2a_sem.at[6]).wait()
+    pltpu.make_async_copy(recv.at[others], recv.at[others], a2a_sem.at[9]).wait()
     for leg in range(3):
         for k in range(chunks):
             sent(k, leg)
@@ -404,10 +430,12 @@
             pltpu.VMEM((D, 2048), BF16),
             pltpu.VMEM((D, 2048), BF16),
             pltpu.VMEM((2, 256, QUART), BF16),
-            pltpu.VMEM((n_seq, 8, QUART), BF16),
-            pltpu.VMEM((n_seq, 8, QUART), BF16),
+            pltpu.VMEM((4, n_seq // 4, 8, QUART), BF16),
+            pltpu.VMEM((4, n_seq // 4, 8, QUART), BF16),
+            pltpu.VMEM((n_seq // 4, 4, 8, QUART), BF16),
             pltpu.VMEM((1, 128), F32),
-            pltpu.VMEM((n_seq, 1, 128), F32),
+            pltpu.VMEM((4, 1, 128), F32),
+            pltpu.VMEM((n_seq // 4, 4, 1, 128), F32),
             pltpu.VMEM((2, 2, 128, HALF), BF16),
             pltpu.VMEM((128, D), BF16),
             pltpu.VMEM((128, HALF), BF16),
@@ -422,7 +450,8 @@
             pltpu.VMEM((4, 64, 256), BF16),
             pltpu.SemaphoreType.REGULAR,
             pltpu.SemaphoreType.DMA((9,)),
-            pltpu.SemaphoreType.DMA((6,)),
+            pltpu.SemaphoreType.DMA((11,)),
+            pltpu.SemaphoreType.DMA((4,)),
             pltpu.SemaphoreType.DMA((3 * chunks,)),
             pltpu.SemaphoreType.DMA((3 * chunks,)),
             pltpu.SemaphoreType.DMA((18,)),

time: 69.6 us -> 68.5 us (0.984)
  Pallas kernels: 68.1 us -> 67 us
    pallas_call x1, Pallas kernels: 68.1 us -> 67 us  [shards(): pl.pallas_call(functools.partial(kernel, n_seq, chunks), name='encoder_la...]
where the time goes in v5:
time: 68.5 us; the launch traced here: 67.7 us
  Pallas kernels  67 us (98%)
    pallas_call x1, Pallas kernels, shards(): pl.pallas_call(functools.partial(kernel, n_seq, chunks), name='encoder_la...  67 us

profile of v5, /device:TPU:1, one launch (start us, length us, event | category | flops | bytes accessed | tf_op | source)
XLA Modules:
  0.0 67.7 jit_solution(3685080224175885208)
XLA Ops:
  0.0 67.0 %encoder_layer.1 = bf16[64,1024]{1,0:T(8,128)(2,1)S(1)} custom-call(s32[1,16]{1,0:T(1,128)} %tile_hbm.1, s32[1,256]{1,0:T(1,128)} %keep_hbm.1, s32[1,256]{1,0:T(1,128)} %slot_hbm.1, f32[1,256]{1,0:T(1,128)} %constant.8.freq_hbm, bf16[1,256,1024]{2,1,0:T(8,128)(2,1)} %patch_hbm.1, bf16[3,1024,512]{2,1,0:T(8,128)(2,1)} %bitcast.5, bf16[1024,1024]{1,0:T(8,128)(2,1)} %out_hbm.1, ...), custom_call_target="tpu_custom_call" | custom-call | tf_op jit(solution)/shard_map/encoder_layer/pallas_call | solution.py:416
  67.0 0.7 copy.11

commit v6 on v5

--- a/solution.py
+++ b/solution.py
@@ -95,8 +95,7 @@
     ]
     for load in index_loads:
         load.start()
-    for load in (patch_load, qkv_load, out_load, up_load, down_load):
-        load.start()
+    patch_load.start()
 
     for load in index_loads:
         load.wait()
@@ -113,6 +112,8 @@
     lab_out[...] = labels[0:1, :]
 
     patch_load.wait()
+    for load in (up_load, down_load, qkv_load, out_load):
+        load.start()
     freq = freq_ref[...]
     within = lax.broadcasted_iota(jnp.int32, (16, QUART), 0)
     cell = jnp.where(c == 0, within // 4, lax.rem(within, 4))
@@ -231,6 +232,13 @@
     own_column = pltpu.make_async_copy(mid.at[:, z], recv.at[z], a2a_sem.at[10])
     own_column.start()
 
+    landed(up_v, f_left, 2, 0)
+    ship(up_v, f_left, 0, f_right, 6)
+    landed(up_v, f_right, 2, 1)
+    ship(up_v, f_right, 1, f_left, 7)
+    ship(down_v, f, 1, f_right, 3)
+    ship(down_v, f, 0, f_left, 4)
+
     others = pl.ds(0, n_z - 1)
     own_labels.wait()
     pltpu.make_async_copy(lab_in.at[others], lab_in.at[others], a2a_sem.at[7]).wait()
@@ -249,13 +257,7 @@
     for h in range(2):
         row_h = jnp.where(half_of == h, row_of, -1)[0:1, :]
         places.append(jnp.where(r_i == row_h, 1.0, 0.0).astype(BF16))
-    landed(up_v, f_left, 2, 0)
-    ship(up_v, f_left, 0, f_right, 6)
-    landed(up_v, f_right, 2, 1)
-    ship(up_v, f_right, 1, f_left, 7)
-    ship(down_v, f, 1, f_right, 3)
-    ship(down_v, f, 0, f_left, 4)
-
+    places = jnp.concatenate(places, axis=0)
     own_column.wait()
     pltpu.make_async_copy(recv.at[others], recv.at[others], a2a_sem.at[3]).wait()
     came_rows = recv[...].reshape(512, QUART)
@@ -281,16 +283,21 @@
 
     pair = {"canvas": other}
     diagonal = {"seq": s_diag, "canvas": other}
+    placed = matmul(places, came_rows).astype(BF16)
     for k in range(chunks):
         for h in range(2):
-            place = places[h][k * size:(k + 1) * size, :]
-            vis[c, c, k * size:(k + 1) * size, h * QUART:(h + 1) * QUART] = matmul(place, came_rows).astype(BF16)
+            part_rows = placed[h * 128 + k * size:h * 128 + (k + 1) * size, :]
+            vis[c, c, k * size:(k + 1) * size, h * QUART:(h + 1) * QUART] = part_rows
         pass_on(c, c, c, k, pair, 0)
     ship(up_v, f_left, 2, mate, 12)
     ship(up_v, f_right, 2, mate, 13)
     for k in range(chunks):
         arrived(other, other, k, 0)
         pass_on(other, other, c, k, diagonal, 1)
+    landed(down_v, f_left, 0, 2)
+    ship(down_v, f_left, 0, f_right, 8)
+    landed(down_v, f_right, 1, 5)
+    ship(down_v, f_right, 1, f_left, 9)
     for k in range(chunks):
         arrived(other, c, k, 1)
         pass_on(other, c, other, k, pair, 2)
@@ -311,10 +318,6 @@
     landed(up_v, f_far, 0, 6)
     landed(up_v, f_far, 1, 7)
     ship(up_v, f_far, 2, mate, 16)
-    landed(down_v, f_left, 0, 2)
-    ship(down_v, f_left, 0, f_right, 8)
-    landed(down_v, f_right, 1, 5)
-    ship(down_v, f_right, 1, f_left, 9)
     for k in range(chunks):
         arrived(c, other, k, 2)
     project(c)
@@ -358,6 +361,10 @@
     resid[...] += mix(other)
     normed2[...] = normalised(resid[...]).astype(BF16)
 
+    landed(down_v, f_far, 0, 8)
+    landed(down_v, f_far, 1, 9)
+    ship(down_v, f_far, 2, mate, 17)
+
     landed(up_v, mate, 2, 10)
     landed(up_v, m_left, 2, 12)
     landed(up_v, m_right, 2, 13)
@@ -369,10 +376,6 @@
         return carry
 
     lax.fori_loop(0, 8, widen, 0)
-
-    landed(down_v, f_far, 0, 8)
-    landed(down_v, f_far, 1, 9)
-    ship(down_v, f_far, 2, mate, 17)
 
     here = pl.ds(pl.multiple_of(c * 64, 64), 64)
     there = pl.ds(pl.multiple_of(other * 64, 64), 64)

time: 68.5 us -> 68.5 us (level)
  the two profiles are of different devices: /device:TPU:1 before, /device:TPU:12 now
where the time goes in v6:
time: 68.5 us; the launch traced here: 68.4 us
  Pallas kernels  67.7 us (99%)
    pallas_call x1, Pallas kernels, shards(): pl.pallas_call(functools.partial(kernel, n_seq, chunks), name='encoder_la...  67.7 us

profile of v6, /device:TPU:12, one launch (start us, length us, event | category | flops | bytes accessed | tf_op | source)
XLA Modules:
  0.0 68.4 jit_solution(15167807891800541945)
XLA Ops:
  0.0 67.7 %encoder_layer.1 = bf16[64,1024]{1,0:T(8,128)(2,1)S(1)} custom-call(s32[1,16]{1,0:T(1,128)} %tile_hbm.1, s32[1,256]{1,0:T(1,128)} %keep_hbm.1, s32[1,256]{1,0:T(1,128)} %slot_hbm.1, f32[1,256]{1,0:T(1,128)} %constant.8.freq_hbm, bf16[1,256,1024]{2,1,0:T(8,128)(2,1)} %patch_hbm.1, bf16[3,1024,512]{2,1,0:T(8,128)(2,1)} %bitcast.5, bf16[1024,1024]{1,0:T(8,128)(2,1)} %out_hbm.1, ...), custom_call_target="tpu_custom_call" | custom-call | tf_op jit(solution)/shard_map/encoder_layer/pallas_call | solution.py:419
  67.7 0.7 copy.11

commit v7 on v6

--- a/solution.py
+++ b/solution.py
@@ -232,13 +232,6 @@
     own_column = pltpu.make_async_copy(mid.at[:, z], recv.at[z], a2a_sem.at[10])
     own_column.start()
 
-    landed(up_v, f_left, 2, 0)
-    ship(up_v, f_left, 0, f_right, 6)
-    landed(up_v, f_right, 2, 1)
-    ship(up_v, f_right, 1, f_left, 7)
-    ship(down_v, f, 1, f_right, 3)
-    ship(down_v, f, 0, f_left, 4)
-
     others = pl.ds(0, n_z - 1)
     own_labels.wait()
     pltpu.make_async_copy(lab_in.at[others], lab_in.at[others], a2a_sem.at[7]).wait()
@@ -258,6 +251,13 @@
         row_h = jnp.where(half_of == h, row_of, -1)[0:1, :]
         places.append(jnp.where(r_i == row_h, 1.0, 0.0).astype(BF16))
     places = jnp.concatenate(places, axis=0)
+    landed(up_v, f_left, 2, 0)
+    ship(up_v, f_left, 0, f_right, 6)
+    landed(up_v, f_right, 2, 1)
+    ship(up_v, f_right, 1, f_left, 7)
+    ship(down_v, f, 1, f_right, 3)
+    ship(down_v, f, 0, f_left, 4)
+
     own_column.wait()
     pltpu.make_async_copy(recv.at[others], recv.at[others], a2a_sem.at[3]).wait()
     came_rows = recv[...].reshape(512, QUART)
@@ -294,14 +294,14 @@
     for k in range(chunks):
         arrived(other, other, k, 0)
         pass_on(other, other, c, k, diagonal, 1)
+    for k in range(chunks):
+        arrived(other, c, k, 1)
+        pass_on(other, c, other, k, pair, 2)
+
     landed(down_v, f_left, 0, 2)
     ship(down_v, f_left, 0, f_right, 8)
     landed(down_v, f_right, 1, 5)
     ship(down_v, f_right, 1, f_left, 9)
-    for k in range(chunks):
-        arrived(other, c, k, 1)
-        pass_on(other, c, other, k, pair, 2)
-
     qkv_load.wait()
 
     def project(block):

time: 68.5 us -> 68.5 us (level)
  the two profiles are of different devices: /device:TPU:12 before, /device:TPU:8 now
where the time goes in v7:
time: 68.5 us; the launch traced here: 68.4 us
  Pallas kernels  67.7 us (99%)
    pallas_call x1, Pallas kernels, shards(): pl.pallas_call(functools.partial(kernel, n_seq, chunks), name='encoder_la...  67.7 us

profile of v7, /device:TPU:8, one launch (start us, length us, event | category | flops | bytes accessed | tf_op | source)
XLA Modules:
  0.0 68.4 jit_solution(16865298104284119636)
XLA Ops:
  0.0 67.7 %encoder_layer.1 = bf16[64,1024]{1,0:T(8,128)(2,1)S(1)} custom-call(s32[1,16]{1,0:T(1,128)} %tile_hbm.1, s32[1,256]{1,0:T(1,128)} %keep_hbm.1, s32[1,256]{1,0:T(1,128)} %slot_hbm.1, f32[1,256]{1,0:T(1,128)} %constant.8.freq_hbm, bf16[1,256,1024]{2,1,0:T(8,128)(2,1)} %patch_hbm.1, bf16[3,1024,512]{2,1,0:T(8,128)(2,1)} %bitcast.5, bf16[1024,1024]{1,0:T(8,128)(2,1)} %out_hbm.1, ...), custom_call_target="tpu_custom_call" | custom-call | tf_op jit(solution)/shard_map/encoder_layer/pallas_call | solution.py:419
  67.7 0.7 copy.11

commit v8 on v7

--- a/solution.py
+++ b/solution.py
@@ -53,30 +53,6 @@
     block_in = lax.rem(s + n_seq - c, n_seq)
     s_diag = lax.rem(s + n_seq + 2 * c - 1, n_seq)
 
-    barrier = pltpu.get_barrier_semaphore()
-    n_z = n_seq // 4
-    z, y_hi = s // 4, lax.rem(s, 4)
-
-    def peer_at(dz, dy):
-        return lax.rem(z + dz + n_z, n_z) * 4 + lax.rem(y_hi + dy, 4)
-
-    def far_first(j, reach):
-        return (reach - (j + 1) // 2) * (1 - 2 * lax.rem(j, 2))
-
-    for dy in (2, 1, 3):
-        pl.semaphore_signal(barrier, inc=1, device_id={"seq": peer_at(0, dy)}, device_id_type=MESH)
-
-    def greet(j, carry):
-        dz = (n_z // 4 - j // 2) * (1 - 2 * lax.rem(j, 2))
-        pl.semaphore_signal(barrier, inc=1, device_id={"seq": peer_at(dz, 0)}, device_id_type=MESH)
-        return carry
-
-    lax.fori_loop(0, n_z // 2, greet, 0)
-    for peer in (f_right, f_left, mate):
-        pl.semaphore_signal(barrier, inc=1, device_id={"fsdp": peer}, device_id_type=MESH)
-    pl.semaphore_signal(barrier, inc=1, device_id={"canvas": other}, device_id_type=MESH)
-    pl.semaphore_signal(barrier, inc=1, device_id={"seq": s_diag, "canvas": other}, device_id_type=MESH)
-
     col0 = pl.multiple_of(c * HALF, HALF)
     patch_load = pltpu.make_async_copy(patch_hbm.at[0, :, pl.ds(col0, HALF)], patch_v, load_sem.at[0])
     qkv_load = pltpu.make_async_copy(qkv_hbm, qkv_v, load_sem.at[1])
@@ -96,6 +72,30 @@
     for load in index_loads:
         load.start()
     patch_load.start()
+
+    barrier = pltpu.get_barrier_semaphore()
+    n_z = n_seq // 4
+    z, y_hi = s // 4, lax.rem(s, 4)
+
+    def peer_at(dz, dy):
+        return lax.rem(z + dz + n_z, n_z) * 4 + lax.rem(y_hi + dy, 4)
+
+    def far_first(j, reach):
+        return (reach - (j + 1) // 2) * (1 - 2 * lax.rem(j, 2))
+
+    for dy in (2, 1, 3):
+        pl.semaphore_signal(barrier, inc=1, device_id={"seq": peer_at(0, dy)}, device_id_type=MESH)
+
+    def greet(j, carry):
+        dz = (n_z // 4 - j // 2) * (1 - 2 * lax.rem(j, 2))
+        pl.semaphore_signal(barrier, inc=1, device_id={"seq": peer_at(dz, 0)}, device_id_type=MESH)
+        return carry
+
+    lax.fori_loop(0, n_z // 2, greet, 0)
+    for peer in (f_right, f_left, mate):
+        pl.semaphore_signal(barrier, inc=1, device_id={"fsdp": peer}, device_id_type=MESH)
+    pl.semaphore_signal(barrier, inc=1, device_id={"canvas": other}, device_id_type=MESH)
+    pl.semaphore_signal(barrier, inc=1, device_id={"seq": s_diag, "canvas": other}, device_id_type=MESH)
 
     for load in index_loads:
         load.wait()
@@ -136,7 +136,7 @@
                 emb[quarter, rows, :] = (tokens + added).astype(BF16)
         return carry
 
-    lax.fori_loop(0, 8, embed, 0)
+    lax.fori_loop(0, 8, embed, 0, unroll=4)
 
     key = jnp.where(kept, target * 4 + lane4, -1000)
     row_i = lax.broadcasted_iota(jnp.int32, (512, QUART), 0)

time: 68.5 us -> 68.7 us (level)
  the two profiles are of different devices: /device:TPU:8 before, /device:TPU:14 now
where the time goes in v8:
time: 68.7 us; the launch traced here: 68.5 us
  Pallas kernels  67.8 us (99%)
    pallas_call x1, Pallas kernels, shards(): pl.pallas_call(functools.partial(kernel, n_seq, chunks), name='encoder_la...  67.8 us

profile of v8, /device:TPU:14, one launch (start us, length us, event | category | flops | bytes accessed | tf_op | source)
XLA Modules:
  0.0 68.5 jit_solution(2473806387037956534)
XLA Ops:
  0.0 67.8 %encoder_layer.1 = bf16[64,1024]{1,0:T(8,128)(2,1)S(1)} custom-call(s32[1,16]{1,0:T(1,128)} %tile_hbm.1, s32[1,256]{1,0:T(1,128)} %keep_hbm.1, s32[1,256]{1,0:T(1,128)} %slot_hbm.1, f32[1,256]{1,0:T(1,128)} %constant.8.freq_hbm, bf16[1,256,1024]{2,1,0:T(8,128)(2,1)} %patch_hbm.1, bf16[3,1024,512]{2,1,0:T(8,128)(2,1)} %bitcast.5, bf16[1024,1024]{1,0:T(8,128)(2,1)} %out_hbm.1, ...), custom_call_target="tpu_custom_call" | custom-call | tf_op jit(solution)/shard_map/encoder_layer/pallas_call | solution.py:419
  67.8 0.7 copy.11
